TPU v7x, 32 devices: a whole 2x2x4 slice. The times are simulated.
32 devices in a mesh: dp: 4 (over z), fsdp: 8 (over y, x, core).
Axes of the slice: x: 2, y: 2, z: 4, core: 2. Of those that a mesh axis runs over, the one named last changes fastest.
Arguments:
- x_given: bfloat16 [65536, 768], P(('dp', 'fsdp')), may hold values from -6 to 6
- cotangent: bfloat16 [65536, 768], P(('dp', 'fsdp')), may hold values from -6 to 6
- norm_gain: bfloat16 [768], P(('dp', 'fsdp')), may hold values from 0.5 to 1.5
- w_qkv: bfloat16 [768, 2304], P(('dp', 'fsdp')), may hold values from -0.3125 to 0.3125
- w_out: bfloat16 [768, 768], P(('dp', 'fsdp')), may hold values from -1.5 to 1.5
- w_ada: bfloat16 [768, 2304], P(('dp', 'fsdp')), may hold values from -0.21875 to 0.21875
- w_up: bfloat16 [768, 3072], P(('dp', 'fsdp')), may hold values from -0.21875 to 0.21875
- w_down: bfloat16 [3072, 768], P(('dp', 'fsdp')), may hold values from -0.15625 to 0.15625
- seq_spans: int32 [128, 2], P(('dp', 'fsdp')), may hold values from 0 to 1024, as said below
- time_steps: int32 [128], P(('dp', 'fsdp')), may hold values from 0 to 999
- page_deal: int32 [4096], replicated, may hold values from 0 to 4095, as said below
Outputs:
- output: bfloat16 [65536, 768], P(('dp', 'fsdp'))
- input_grad: bfloat16 [65536, 768], P(('dp', 'fsdp'))
- gain_grad: float32 [768], P(('dp', 'fsdp'))
- qkv_grad: float32 [768, 2304], P(('dp', 'fsdp'))
- out_grad: float32 [768, 768], P(('dp', 'fsdp'))
- ada_grad: float32 [768, 2304], P(('dp', 'fsdp'))
- up_grad: float32 [768, 3072], P(('dp', 'fsdp'))
- down_grad: float32 [3072, 768], P(('dp', 'fsdp'))
Inputs may be any that keep to these rules, and one draw needn't show every extreme that they name: seq_spans[j] = (start, length) of slot j, rows start to start + length - 1 of bin j // 2; slots of one bin don't intersect and end by 1024; a length may be 0; some bin holds one sequence of 1024 tokens. page_deal is a permutation; of the pages that one device holds in given order, the same number goes to every device.
All inputs are finite; a program needn't handle non-finite values.
Results may differ from a plain program's by a relative error of at most 0.014.
Values may be sent and summed in bfloat16 or wider, within the bound.
A program may use at most 320 MiB of HBM per device.

v0:
```python
import math

import jax
import jax.numpy as jnp
from jax import lax
from jax.sharding import PartitionSpec as P

D = 768
HEADS = 12
HEAD = 64
FF = 3072
BIN = 1024
MB = 2
SLOTS = 2
PAGE = 16


eps = 1e-05
neg_big = -1e30
highest = lax.Precision.HIGHEST
rows_contract = (((0,), (0,)), ((), ()))
cols_contract = (((1,), (1,)), ((), ()))


def layer_norm(values, gain_vec):
    center = jnp.mean(values, axis=-1, keepdims=True)
    shifted = values - center
    spread = jnp.mean(shifted * shifted, axis=-1, keepdims=True)
    return shifted * lax.rsqrt(spread + eps) * gain_vec


def modulate(values, scale_rows, shift_rows):
    center = jnp.mean(values, axis=-1, keepdims=True)
    shifted = values - center
    spread = jnp.mean(shifted * shifted, axis=-1, keepdims=True)
    return shifted * lax.rsqrt(spread + eps) * (1.0 + scale_rows) + shift_rows


def gelu_tanh(values):
    return jax.nn.gelu(values, approximate=True)


def rope_tables(position, head_size):
    half_size = head_size // 2
    frequency = jnp.exp(jnp.arange(half_size, dtype=jnp.float32) * (-math.log(10000.0) / half_size))
    angles = position[:, None] * frequency[None, :]
    return (jnp.cos(angles), jnp.sin(angles))


def rotate(values, cosine, sine_table):
    half_size = values.shape[-1] // 2
    first_half = values[..., :half_size]
    second = values[..., half_size:]
    cos_rows = cosine[:, None, :]
    sin_rows = sine_table[:, None, :]
    return jnp.concatenate(
        [first_half * cos_rows - second * sin_rows, second * cos_rows + first_half * sin_rows],
        axis=-1,
    )


def unrotate(values, cosine, sine_table):
    half_size = values.shape[-1] // 2
    first_half = values[..., :half_size]
    second = values[..., half_size:]
    cos_rows = cosine[:, None, :]
    sin_rows = sine_table[:, None, :]
    return jnp.concatenate(
        [first_half * cos_rows + second * sin_rows, second * cos_rows - first_half * sin_rows],
        axis=-1,
    )


def time_features(time_steps, width):
    half_size = width // 2
    frequency = jnp.exp(jnp.arange(half_size, dtype=jnp.float32) * (-math.log(10000.0) / half_size))
    angles = time_steps.astype(jnp.float32)[:, None] * frequency[None, :]
    return jnp.concatenate([jnp.cos(angles), jnp.sin(angles)], axis=-1)


def row_layout(seq_spans, row_count):
    row_index = jnp.arange(row_count, dtype=jnp.int32)
    starts = seq_spans[:, 0]
    lengths = seq_spans[:, 1]
    offset = row_index[:, None] - starts[None, :]
    member = (offset >= 0) & (offset < lengths[None, :])
    slot_onehot = member.astype(jnp.float32)
    live_rows = jnp.sum(slot_onehot, axis=1)
    slot_ids = jnp.arange(seq_spans.shape[0], dtype=jnp.int32)
    segment = jnp.sum(jnp.where(member, slot_ids[None, :], 0), axis=1) - jnp.where(
        jnp.any(member, axis=1), 0, 1
    )
    position = jnp.sum(jnp.where(member, offset, 0), axis=1).astype(jnp.float32)
    allowed = (segment[:, None] == segment[None, :]) & (segment[:, None] >= 0) | (
        row_index[:, None] == row_index[None, :]
    )
    return (slot_onehot, live_rows, position, allowed)


def head_scores(query_head, key_head, allowed):
    scores = (
        lax.dot_general(query_head, key_head, cols_contract, preferred_element_type=jnp.float32)
        * 0.125
    )
    return jnp.where(allowed, scores, neg_big)


def attend(query_head, key_head, value_head, allowed):
    masked = head_scores(query_head, key_head, allowed)
    row_max = jnp.max(masked, axis=1, keepdims=True)
    log_total = row_max + jnp.log(jnp.sum(jnp.exp(masked - row_max), axis=1, keepdims=True))
    probs_low = jnp.exp(masked - log_total).astype(jnp.bfloat16)
    return (jnp.dot(probs_low, value_head, preferred_element_type=jnp.float32), log_total[:, 0])


def attend_back(query_head, key_head, value_head, dout_head, log_total, allowed):
    masked = head_scores(query_head, key_head, allowed)
    probs = jnp.exp(masked - log_total[:, None])
    probs_low = probs.astype(jnp.bfloat16)
    dprobs = lax.dot_general(
        dout_head, value_head, cols_contract, preferred_element_type=jnp.float32
    )
    inner = jnp.sum(probs * dprobs, axis=1, keepdims=True)
    dscores_low = (probs * (dprobs - inner)).astype(jnp.bfloat16)
    dquery = jnp.dot(dscores_low, key_head, preferred_element_type=jnp.float32) * 0.125
    dkey = (
        lax.dot_general(dscores_low, query_head, rows_contract, preferred_element_type=jnp.float32)
        * 0.125
    )
    dvalue = lax.dot_general(
        probs_low, dout_head, rows_contract, preferred_element_type=jnp.float32
    )
    return (dquery, dkey, dvalue)


def per_device(
    x_given,
    cotangent,
    norm_gain,
    w_qkv,
    w_out,
    w_ada,
    w_up,
    w_down,
    seq_spans,
    time_steps,
    page_deal,
):
    shards = lax.axis_size(("dp", "fsdp"))
    device = lax.axis_index(("dp", "fsdp"))
    rows_dev, width = x_given.shape
    pages_dev = rows_dev // PAGE
    per_peer = pages_dev // shards
    page_ids = jnp.arange(pages_dev, dtype=jnp.int32)
    local_deal = lax.dynamic_slice_in_dim(page_deal, device * pages_dev, pages_dev)
    target = local_deal // pages_dev
    earlier = (target[:, None] == target[None, :]) & (local_deal[None, :] < local_deal[:, None])
    send_pos = target * per_peer + jnp.sum(earlier.astype(jnp.int32), axis=1)
    send_order = jnp.zeros((pages_dev,), jnp.int32).at[send_pos].set(page_ids)
    page_total = page_deal.shape[0]
    inverse = (
        jnp.zeros((page_total,), jnp.int32)
        .at[page_deal]
        .set(jnp.arange(page_total, dtype=jnp.int32))
    )
    owned_pages = lax.dynamic_slice_in_dim(inverse, device * pages_dev, pages_dev)
    source = owned_pages // pages_dev
    before = (source[:, None] == source[None, :]) & (page_ids[None, :] < page_ids[:, None])
    recv_pos = source * per_peer + jnp.sum(before.astype(jnp.int32), axis=1)
    send_x = x_given.reshape(pages_dev, PAGE, width)[send_order].reshape(
        shards, per_peer, PAGE, width
    )
    send_dy = cotangent.reshape(pages_dev, PAGE, width)[send_order].reshape(
        shards, per_peer, PAGE, width
    )
    got_x, got_dy = (
        lax.all_to_all(send_x, ("dp", "fsdp"), split_axis=0, concat_axis=0, tiled=True),
        lax.all_to_all(send_dy, ("dp", "fsdp"), split_axis=0, concat_axis=0, tiled=True),
    )
    dealt_x = got_x.reshape(shards * per_peer, PAGE, width)[recv_pos].reshape(rows_dev, width)
    dealt_dy = got_dy.reshape(shards * per_peer, PAGE, width)[recv_pos].reshape(rows_dev, width)
    grad_sums = (
        jnp.zeros((D,), jnp.float32),
        jnp.zeros((D, 3 * D), jnp.float32),
        jnp.zeros((D, D), jnp.float32),
        jnp.zeros((D, 3 * D), jnp.float32),
        jnp.zeros((D, FF), jnp.float32),
        jnp.zeros((FF, D), jnp.float32),
    )
    output_parts = []
    grad_parts = []
    for micro_step in range(MB):
        x_bin = dealt_x[micro_step * BIN : (micro_step + 1) * BIN].astype(jnp.float32)
        dy_bin = dealt_dy[micro_step * BIN : (micro_step + 1) * BIN].astype(jnp.float32)
        spans_bin = seq_spans[micro_step * SLOTS : (micro_step + 1) * SLOTS]
        steps_bin = time_steps[micro_step * SLOTS : (micro_step + 1) * SLOTS]
        fetched = (
            lax.all_gather(norm_gain, ("dp", "fsdp"), axis=0, tiled=True),
            lax.all_gather(w_qkv, ("dp", "fsdp"), axis=0, tiled=True),
            lax.all_gather(w_out, ("dp", "fsdp"), axis=0, tiled=True),
            lax.all_gather(w_ada, ("dp", "fsdp"), axis=0, tiled=True),
            lax.all_gather(w_up, ("dp", "fsdp"), axis=0, tiled=True),
            lax.all_gather(w_down, ("dp", "fsdp"), axis=0, tiled=True),
        )
        gain_all, qkv_all, proj_all, ada_all, up_all, down_all = fetched
        slot_onehot, live_rows, position, allowed = row_layout(spans_bin, BIN)
        time_feat = time_features(steps_bin, width).astype(jnp.bfloat16)
        ada_seq = jnp.dot(time_feat, ada_all, preferred_element_type=jnp.float32)
        ada_rows = jnp.sum(slot_onehot[:, :, None] * ada_seq[None, :, :], axis=1)
        scale_rows = ada_rows[:, :width]
        shift_rows = ada_rows[:, width : 2 * width]
        gate_rows = ada_rows[:, 2 * width :]
        normed, norm_back = jax.vjp(layer_norm, x_bin, gain_all.astype(jnp.float32))
        normed_low = normed.astype(jnp.bfloat16)
        mixed_qkv = jnp.dot(normed_low, qkv_all, preferred_element_type=jnp.float32)
        cosine, sine_table = rope_tables(position, HEAD)
        query_low = rotate(
            mixed_qkv[:, :width].reshape(BIN, HEADS, HEAD), cosine, sine_table
        ).astype(jnp.bfloat16)
        key_low = rotate(
            mixed_qkv[:, width : 2 * width].reshape(BIN, HEADS, HEAD), cosine, sine_table
        ).astype(jnp.bfloat16)
        value_low = mixed_qkv[:, 2 * width :].reshape(BIN, HEADS, HEAD).astype(jnp.bfloat16)
        query_heads = jnp.transpose(query_low, (1, 0, 2))
        key_heads = jnp.transpose(key_low, (1, 0, 2))
        value_heads = jnp.transpose(value_low, (1, 0, 2))

        def forward_head(block):
            return attend(block[0], block[1], block[2], allowed)

        head_out, log_total = lax.map(forward_head, (query_heads, key_heads, value_heads))
        attended = jnp.transpose(head_out, (1, 0, 2)).reshape(BIN, width).astype(jnp.bfloat16)
        residual = x_bin + jnp.dot(attended, proj_all, preferred_element_type=jnp.float32)
        hidden_in, mod_back = jax.vjp(modulate, residual, scale_rows, shift_rows)
        hidden_low = hidden_in.astype(jnp.bfloat16)
        pre_act = jnp.dot(hidden_low, up_all, preferred_element_type=jnp.float32)
        activation, gelu_back = jax.vjp(gelu_tanh, pre_act)
        activ_low = activation.astype(jnp.bfloat16)
        branch = jnp.dot(activ_low, down_all, preferred_element_type=jnp.float32)
        output_parts.append(
            ((residual + gate_rows * branch) * live_rows[:, None]).astype(jnp.bfloat16)
        )
        back_qkv, back_proj, back_up, back_down = (
            lax.all_gather(w_qkv, ("dp", "fsdp"), axis=0, tiled=True),
            lax.all_gather(w_out, ("dp", "fsdp"), axis=0, tiled=True),
            lax.all_gather(w_up, ("dp", "fsdp"), axis=0, tiled=True),
            lax.all_gather(w_down, ("dp", "fsdp"), axis=0, tiled=True),
        )
        dy_live = dy_bin * live_rows[:, None]
        gate_grad = dy_live * branch
        dbranch_low = (dy_live * gate_rows).astype(jnp.bfloat16)
        down_term = lax.dot_general(
            activ_low, dbranch_low, rows_contract, preferred_element_type=jnp.float32
        )
        dactiv = lax.dot_general(
            dbranch_low, back_down, cols_contract, preferred_element_type=jnp.float32
        )
        dpre_low = gelu_back(dactiv)[0].astype(jnp.bfloat16)
        up_term = lax.dot_general(
            hidden_low, dpre_low, rows_contract, preferred_element_type=jnp.float32
        )
        dhidden = lax.dot_general(
            dpre_low, back_up, cols_contract, preferred_element_type=jnp.float32
        )
        dresid_norm, scale_grad, shift_grad = mod_back(dhidden)
        dresid = dy_live + dresid_norm
        dada_rows = jnp.concatenate([scale_grad, shift_grad, gate_grad], axis=1)
        dada_seq = jnp.dot(slot_onehot.T, dada_rows, precision=highest)
        ada_term = jnp.dot(time_feat.astype(jnp.float32).T, dada_seq, precision=highest)
        dattn_low = dresid.astype(jnp.bfloat16)
        proj_term = lax.dot_general(
            attended, dattn_low, rows_contract, preferred_element_type=jnp.float32
        )
        dattended = lax.dot_general(
            dattn_low, back_proj, cols_contract, preferred_element_type=jnp.float32
        ).astype(jnp.bfloat16)
        dout_heads = jnp.transpose(dattended.reshape(BIN, HEADS, HEAD), (1, 0, 2))

        def backward_head(block):
            return attend_back(block[0], block[1], block[2], block[3], block[4], allowed)

        dq_heads, dk_heads, dv_heads = lax.map(
            backward_head, (query_heads, key_heads, value_heads, dout_heads, log_total)
        )
        dq_rows = unrotate(jnp.transpose(dq_heads, (1, 0, 2)), cosine, sine_table).reshape(
            BIN, width
        )
        dk_rows = unrotate(jnp.transpose(dk_heads, (1, 0, 2)), cosine, sine_table).reshape(
            BIN, width
        )
        dv_rows = jnp.transpose(dv_heads, (1, 0, 2)).reshape(BIN, width)
        dmixed_low = jnp.concatenate([dq_rows, dk_rows, dv_rows], axis=1).astype(jnp.bfloat16)
        qkv_term = lax.dot_general(
            normed_low, dmixed_low, rows_contract, preferred_element_type=jnp.float32
        )
        dnormed = lax.dot_general(
            dmixed_low, back_qkv, cols_contract, preferred_element_type=jnp.float32
        )
        dx_norm, gain_term = norm_back(dnormed)
        grad_parts.append((dresid + dx_norm).astype(jnp.bfloat16))
        new_terms = (gain_term, qkv_term, proj_term, ada_term, up_term, down_term)
        grad_sums = tuple((running + adding for running, adding in zip(grad_sums, new_terms)))
    gain_grad, qkv_grad, out_grad, ada_grad, up_grad, down_grad = lax.psum_scatter(
        grad_sums, ("dp", "fsdp"), scatter_dimension=0, tiled=True
    )
    out_dealt = jnp.concatenate(output_parts, axis=0).reshape(pages_dev, PAGE, width)
    dx_dealt = jnp.concatenate(grad_parts, axis=0).reshape(pages_dev, PAGE, width)
    back_out = (
        jnp.zeros_like(out_dealt).at[recv_pos].set(out_dealt).reshape(shards, per_peer, PAGE, width)
    )
    back_dx = (
        jnp.zeros_like(dx_dealt).at[recv_pos].set(dx_dealt).reshape(shards, per_peer, PAGE, width)
    )
    ret_out, ret_dx = (
        lax.all_to_all(back_out, ("dp", "fsdp"), split_axis=0, concat_axis=0, tiled=True),
        lax.all_to_all(back_dx, ("dp", "fsdp"), split_axis=0, concat_axis=0, tiled=True),
    )
    output = ret_out.reshape(shards * per_peer, PAGE, width)[send_pos].reshape(rows_dev, width)
    input_grad = ret_dx.reshape(shards * per_peer, PAGE, width)[send_pos].reshape(rows_dev, width)
    return (output, input_grad, gain_grad, qkv_grad, out_grad, ada_grad, up_grad, down_grad)


def solution(mesh):
    placed = (
        P(("dp", "fsdp"), None),
        P(("dp", "fsdp"), None),
        P(("dp", "fsdp")),
        P(("dp", "fsdp"), None),
        P(("dp", "fsdp"), None),
        P(("dp", "fsdp"), None),
        P(("dp", "fsdp"), None),
        P(("dp", "fsdp"), None),
        P(("dp", "fsdp"), None),
        P(("dp", "fsdp")),
        P(),
    )
    return jax.shard_map(
        per_device,
        mesh=mesh,
        in_specs=placed,
        out_specs=(
            P(("dp", "fsdp"), None),
            P(("dp", "fsdp"), None),
            P(("dp", "fsdp")),
            P(("dp", "fsdp"), None),
            P(("dp", "fsdp"), None),
            P(("dp", "fsdp"), None),
            P(("dp", "fsdp"), None),
            P(("dp", "fsdp"), None),
        ),
        check_vma=False,
    )
```

profile of v0, /device:TPU:0, one launch (start us, length us, event | category | flops | bytes accessed | tf_op | source)
XLA Modules:
  0.0 1707.4 jit_solution(17528368974200104684)
XLA Ops:
  10.7 15.5 scatter_custom_fusion
  30.7 7.3 all-to-all-start
  42.4 83.5 %all-to-all-done = bf16[32,4,16,768]{3,2,1,0:T(8,128)(2,1)S(1)} async-done(((bf16[32,4,16,768]{3,2,1,0:T(8,128)(2,1)}), bf16[32,4,16,768]{3,2,1,0:T(8,128)(2,1)S(1)}, u32[]{:S(2)}, u32[]{:S(2)}) %all-to-all-start) | async-done | bytes 3145760 | tf_op jit(solution)/shard_map/all_to_all | solution.py:177
  142.0 93.2 %all-reduce = bf16[768]{0:T(1024)(128)(2,1)S(1)} all-reduce(bf16[768]{0:T(1024)(128)(2,1)S(1)} %dynamic-update-slice), channel_id=1, replica_groups=mesh['dp'=4,'fsdp'=8] {'dp','fsdp'}, use_global_device_ids=true, to_apply=%add | all-reduce | flops 768 | bytes 3072
  282.7 7.0 fusion.160
  335.5 64.4 %while.57 = (s32[]{:T(128)}, bf16[12,1024,64]{1,2,0:T(8,128)(2,1)}, f32[12,1024]{1,0:T(8,128)S(1)}, bf16[12,1024,64]{2,1,0:T(8,128)(2,1)}, bf16[12,1024,64]{2,1,...) while((s32[]{:T(128)}, bf16[12,1024,64]{1,2,0:T(8,128)(2,1)}, ...), condition=%wide.region_25.26_spmd.clone, body=%wide.region_22.25_spmd.clone.sunk | while | flops 279968768 | bytes 13679721 | solution.py:231
  431.0 64.2 %while.56 = (s32[]{:T(128)}, bf16[12,1024,64]{1,2,0:T(8,128)(2,1)}, f32[12,1024]{1,0:T(8,128)S(1)}, bf16[12,1024,64]{2,1,0:T(8,128)(2,1)}, bf16[12,1024,64]{2,1,...) while((s32[]{:T(128)}, bf16[12,1024,64]{1,2,0:T(8,128)(2,1)}, ...), condition=%wide.region_12.13_spmd.clone, body=%wide.region_9.12_spmd.clone.sunk | while | flops 279968768 | bytes 13679721 | solution.py:231
  558.5 10.3 fusion.174
  568.8 18.5 %fusion.113 = bf16[1024,3072]{1,0:T(8,128)(2,1)} fusion(f32[1024,3072]{1,0:T(8,128)} %fusion.174, bf16[1024,768]{0,1:T(8,128)(2,1)} %multiply_convert_fusion.4, bf16[3072,768]{1,0:T(8,128)(2,1)} %all-gather.14.cloned.1.call-done), kind=kOutput, calls=%fused_computation.141 | convolution fusion | flops 4894752768 | bytes 25165824 | tf_op jit(solution)/shard_map/dot_general | solution.py:255
  587.4 7.9 multiply_reduce_fusion.7
  610.6 163.5 %while.59 = (s32[]{:T(128)}, f32[12,1024,64]{1,2,0:T(8,128)}, f32[12,1024,64]{1,2,0:T(8,128)}, bf16[12,1024,64]{1,2,0:T(8,128)(2,1)}, bf16[12,1024,64]{2,1,0:T(8...) while((s32[]{:T(128)}, f32[12,1024,64]{1,2,0:T(8,128)}, ...), condition=%wide.region_42.43_spmd.clone, body=%wide.region_40.42_spmd.clone.sunk | while | flops 684850176 | bytes 46696624 | solution.py:282
  774.1 14.8 multiply_convert_fusion.3
  789.0 15.9 fusion.106
  804.9 7.7 multiply_reduce_fusion.9
  832.8 169.8 %while.58 = (s32[]{:T(128)}, f32[12,1024,64]{1,2,0:T(8,128)}, f32[12,1024,64]{1,2,0:T(8,128)}, bf16[12,1024,64]{1,2,0:T(8,128)(2,1)}, bf16[12,1024,64]{2,1,0:T(8...) while((s32[]{:T(128)}, f32[12,1024,64]{1,2,0:T(8,128)}, ...), condition=%wide.region_35.36_spmd.clone, body=%wide.region_33.35_spmd.clone.sunk | while | flops 684850176 | bytes 34113656 | solution.py:282
  1019.6 7.1 multiply_reduce_fusion.5
  1033.3 18.1 %multiply_multiply_fusion.6 = (f32[1024,768]{0,1:T(8,128)}, bf16[1024,768]{0,1:T(8,128)(2,1)}, bf16[1024,768]{0,1:T(8,128)(2,1)}) fusion(f32[1024,768]{0,1:T(8,128)} %copy.150, f32[1024]{0:T(1024)S(1)} %copy-done.63, f32[1024]{0:T(1024)S(1)} %negate_multiply_fusion, f32[1024]{0:T(1024)S(1)} %multiply_multiply_fusion.8, f32[1024,768]{0,1:T(8,128)} %copy.138, ...), kind=kOutput, calls=%fused_computation.196 | convolution fusion | flops 4873519104 | bytes 42494976 | tf_op jit(solution)/shard_map/dot_general | solution.py:239
  1058.4 15.2 multiply_multiply_fusion.7
  1073.6 7.0 fusion.114
  1089.1 7.5 fusion.127
  1096.6 8.3 convolution_add_fusion.1
  1106.3 7.6 fusion.177
  1113.9 13.9 convolution_add_fusion.2
  1129.2 7.1 fusion.176
  1136.4 10.3 convolution_add_fusion.3
  1155.0 16.5 scatter_fusion.1
  1186.9 18.4 %scatter_fusion = bf16[128,16,768]{2,1,0:T(8,128)(2,1)} fusion(bf16[128,16,768]{2,1,0:T(8,128)(2,1)} %broadcast.415.clone, s32[128]{0:T(128)S(1)} %copy-done.98, bf16[128,16,768]{2,1,0:T(8,128)(2,1)} %bitcast.305), kind=kCustom, calls=%fused_computation.8 | custom fusion | bytes 9437696 | tf_op jit(solution)/shard_map/scatter | solution.py:309
  1205.3 70.7 %all-to-all-done.3 = bf16[32,4,16,768]{3,2,1,0:T(8,128)(2,1)S(1)} async-done(((bf16[32,4,16,768]{3,2,1,0:T(8,128)(2,1)}), bf16[32,4,16,768]{3,2,1,0:T(8,128)(2,1)S(1)}, u32[]{:S(2)}, u32[]{:S(2)}) %all-to-all-start.3) | async-done | bytes 3145760 | tf_op jit(solution)/shard_map/all_to_all | solution.py:316
  1281.4 100.9 %all-reduce.1 = f32[768]{0:T(1024)S(1)} all-reduce(f32[768]{0:T(1024)S(1)} %add.273), channel_id=2, replica_groups=mesh['dp'=4,'fsdp'=8] {'dp','fsdp'}, use_global_device_ids=true, to_apply=%region_48.49.clone | all-reduce | flops 768 | bytes 6144
  1389.8 27.4 %reduce-scatter.6.cloned.1.call-done = f32[24,2304]{1,0:T(8,128)} async-done(((f32[768,2304]{1,0:T(8,128)}), f32[24,2304]{1,0:T(8,128)}) %reduce-scatter.6.cloned.1.call-update) | async-done | bytes 221200 | tf_op jit(solution)/shard_map/reduce_scatter | solution.py:303
  1417.2 141.7 %reduce-scatter.14.cloned.1.call-done = f32[96,768]{1,0:T(8,128)} async-done(((f32[3072,768]{1,0:T(8,128)}), f32[96,768]{1,0:T(8,128)}) %reduce-scatter.14.cloned.1.call-update) | async-done | bytes 294928 | tf_op jit(solution)/shard_map/reduce_scatter | solution.py:303
  1558.9 141.4 %reduce-scatter.12.cloned.1.call-done = f32[24,3072]{1,0:T(8,128)} async-done(((f32[768,3072]{1,0:T(8,128)}), f32[24,3072]{1,0:T(8,128)}) %reduce-scatter.12.cloned.1.call-update) | async-done | bytes 294928 | tf_op jit(solution)/shard_map/reduce_scatter | solution.py:303
  (763 shorter events, 789.0 us)
Async XLA Ops:
  7.2 21.1 %copy-start = (bf16[2048,768]{1,0:T(8,128)(2,1)S(1)}, bf16[2048,768]{1,0:T(8,128)(2,1)}, u32[]{:S(2)}) copy-start(bf16[2048,768]{1,0:T(8,128)(2,1)} %param.19) | copy-start | bytes 9437188
  7.2 275.5 %all-gather.6.cloned.1.call-start = ((), (), s32[]{:S(2)}) async-start(), calls=%async_computation.9 | async-start | bytes 3649536 | tf_op jit(solution)/shard_map/all_gather | solution.py:199
  7.9 487.4 %all-gather.10.cloned.1.call-start = ((), (), s32[]{:S(2)}) async-start(), calls=%async_computation.11 | async-start | bytes 3649536 | tf_op jit(solution)/shard_map/all_gather | solution.py:201
  8.7 523.8 %all-gather.8.cloned.1.call-start = ((), (), s32[]{:S(2)}) async-start(), calls=%async_computation.10 | async-start | bytes 1216512 | tf_op jit(solution)/shard_map/all_gather | solution.py:200
  9.4 549.1 %all-gather.12.cloned.1.call-start = ((), (), s32[]{:S(2)}) async-start(), calls=%async_computation.12 | async-start | bytes 4866048 | tf_op jit(solution)/shard_map/all_gather | solution.py:202
  30.7 95.2 %all-to-all-start = ((bf16[32,4,16,768]{3,2,1,0:T(8,128)(2,1)}), bf16[32,4,16,768]{3,2,1,0:T(8,128)(2,1)S(1)}, u32[]{:S(2)}, u32[]{:S(2)}) async-start(bf16[32,4,16,768]{3,2,1,0:T(8,128)(2,1)} %bitcast.299), calls=%async_computation | async-start | bytes 6291456 | tf_op jit(solution)/shard_map/all_to_all | solution.py:177
  127.5 138.4 %all-to-all-start.2 = ((bf16[32,4,16,768]{3,2,1,0:T(8,128)(2,1)}), bf16[32,4,16,768]{3,2,1,0:T(8,128)(2,1)}, u32[]{:S(2)}, u32[]{:S(2)}) async-start(bf16[32,4,16,768]{3,2,1,0:T(8,128)(2,1)} %bitcast.30), calls=%async_computation.2 | async-start | bytes 6291456 | tf_op jit(solution)/shard_map/all_to_all | solution.py:178
  131.8 437.0 %all-gather.14.cloned.1.call-start = ((), (), s32[]{:S(2)}) async-start(), calls=%async_computation.13 | async-start | bytes 4866048 | tf_op jit(solution)/shard_map/all_gather | solution.py:203
  132.4 1257.4 %reduce-scatter.8.cloned.1.call-start = ((), (), s32[]{:S(2)}) async-start(), calls=%async_computation.15 | async-start | bytes 2433024 | tf_op jit(solution)/shard_map/reduce_scatter | solution.py:303
  136.4 99.4 %copy-start.107 = (s32[4,2]{0,1:T(2,128)S(1)}, s32[4,2]{0,1:T(2,128)}, u32[]{:S(2)}) copy-start(s32[4,2]{0,1:T(2,128)} %param.27) | copy-start | bytes 100
  136.4 100.6 %copy-start.108 = (s32[4]{0:T(128)S(1)}, s32[4]{0:T(128)}, u32[]{:S(2)}) copy-start(s32[4]{0:T(128)} %param.28) | copy-start | bytes 52
  241.5 69.8 %copy-start.51 = (f32[1024,32]{0,1:T(8,128)}, f32[1024,32]{0,1:T(8,128)S(1)}, u32[]{:S(2)}) copy-start(f32[1024,32]{0,1:T(8,128)S(1)} %get-tuple-element.621) | copy-start | bytes 393220
  241.5 69.8 %copy-start.53 = (f32[1024,32]{0,1:T(8,128)}, f32[1024,32]{0,1:T(8,128)S(1)}, u32[]{:S(2)}) copy-start(f32[1024,32]{0,1:T(8,128)S(1)} %get-tuple-element.622) | copy-start | bytes 393220
  241.5 165.6 %copy-start.55 = (f32[1024,32]{0,1:T(8,128)}, f32[1024,32]{0,1:T(8,128)S(1)}, u32[]{:S(2)}) copy-start(f32[1024,32]{0,1:T(8,128)S(1)} %get-tuple-element.601) | copy-start | bytes 393220
  250.2 32.5 %copy-start.73 = (f32[1024]{0:T(1024)}, f32[1024]{0:T(1024)S(1)}, u32[]{:S(2)}) copy-start(f32[1024]{0:T(1024)S(1)} %div.109) | copy-start | bytes 12292
  274.5 269.4 %copy-start.2 = (f32[1024,768]{0,1:T(8,128)}, f32[1024,768]{0,1:T(8,128)S(1)}, u32[]{:S(2)}) copy-start(f32[1024,768]{0,1:T(8,128)S(1)} %copy.144) | copy-start | bytes 9437188
  431.0 64.3 %copy-start.80 = (bf16[2,384]{1,0:T(2,128)(2,1)S(1)}, bf16[2,384]{1,0:T(2,128)(2,1)}, u32[]{:S(2)}) copy-start(bf16[2,384]{1,0:T(2,128)(2,1)} %get-tuple-element.609) | copy-start | bytes 4612
  431.0 64.3 %copy-start.82 = (bf16[2,384]{1,0:T(2,128)(2,1)S(1)}, bf16[2,384]{1,0:T(2,128)(2,1)}, u32[]{:S(2)}) copy-start(bf16[2,384]{1,0:T(2,128)(2,1)} %get-tuple-element.610) | copy-start | bytes 4612
  568.8 18.6 %copy-start.9 = (f32[1024,768]{0,1:T(8,128)S(1)}, f32[1024,768]{0,1:T(8,128)}, u32[]{:S(2)}) copy-start(f32[1024,768]{0,1:T(8,128)} %copy-done.8) | copy-start | bytes 9437188
  568.8 18.6 %copy-start.14 = (f32[1024,768]{0,1:T(8,128)S(1)}, f32[1024,768]{0,1:T(8,128)}, u32[]{:S(2)}) copy-start(f32[1024,768]{0,1:T(8,128)} %copy.169) | copy-start | bytes 9437188
  568.8 18.6 %copy-start.31 = (bf16[768,3072]{1,0:T(8,128)(2,1)S(1)}, bf16[768,3072]{1,0:T(8,128)(2,1)}, u32[]{:S(2)}) copy-start(bf16[768,3072]{1,0:T(8,128)(2,1)} %all-gather.12.cloned.1.call-done) | copy-start | bytes 14155780
  774.1 30.7 %slice-start = ((s8[4718592]{0:T(1024)(128)(4,1)}), s8[4194304]{0:T(1024)(128)(4,1)S(1)}, s32[]{:S(2)}) async-start(s8[4718592]{0:T(1024)(128)(4,1)} %bitcast.316), calls=%async_computation.19 | async-start | bytes 8388608
  832.8 169.9 %copy-start.56 = (f32[1024,32]{0,1:T(8,128)S(1)}, f32[1024,32]{0,1:T(8,128)}, u32[]{:S(2)}) copy-start(f32[1024,32]{0,1:T(8,128)} %copy-done.55) | copy-start | bytes 393220
  832.8 169.9 %copy-start.58 = (f32[1024,32]{0,1:T(8,128)S(1)}, f32[1024,32]{0,1:T(8,128)}, u32[]{:S(2)}) copy-start(f32[1024,32]{0,1:T(8,128)} %get-tuple-element.602) | copy-start | bytes 393220
  1033.2 18.2 %copy-start.93 = (s32[2]{0:T(128)S(1)}, s32[2]{0:T(128)}, u32[]{:S(2)}) copy-start(s32[2]{0:T(128)} %copy-done.92) | copy-start | bytes 28
  1033.2 356.6 %reduce-scatter.10.cloned.1.call-start = ((), (), s32[]{:S(2)}) async-start(), calls=%async_computation.16 | async-start | bytes 7299072 | tf_op jit(solution)/shard_map/reduce_scatter | solution.py:303
  1089.0 328.2 %reduce-scatter.6.cloned.1.call-start = ((), (), s32[]{:S(2)}) async-start(), calls=%async_computation.14 | async-start | bytes 7299072 | tf_op jit(solution)/shard_map/reduce_scatter | solution.py:303
  1104.9 454.0 %reduce-scatter.14.cloned.1.call-start = ((), (), s32[]{:S(2)}) async-start(), calls=%async_computation.18 | async-start | bytes 9732096 | tf_op jit(solution)/shard_map/reduce_scatter | solution.py:303
  1127.8 572.5 %reduce-scatter.12.cloned.1.call-start = ((), (), s32[]{:S(2)}) async-start(), calls=%async_computation.17 | async-start | bytes 9732096 | tf_op jit(solution)/shard_map/reduce_scatter | solution.py:303
  1171.5 104.5 %all-to-all-start.3 = ((bf16[32,4,16,768]{3,2,1,0:T(8,128)(2,1)}), bf16[32,4,16,768]{3,2,1,0:T(8,128)(2,1)S(1)}, u32[]{:S(2)}, u32[]{:S(2)}) async-start(bf16[32,4,16,768]{3,2,1,0:T(8,128)(2,1)} %bitcast.53), calls=%async_computation.3 | async-start | bytes 6291456 | tf_op jit(solution)/shard_map/all_to_all | solution.py:316
  1276.0 109.3 %all-to-all-start.1 = ((bf16[32,4,16,768]{3,2,1,0:T(8,128)(2,1)}), bf16[32,4,16,768]{3,2,1,0:T(8,128)(2,1)}, u32[]{:S(2)}, u32[]{:S(2)}) async-start(bf16[32,4,16,768]{3,2,1,0:T(8,128)(2,1)} %bitcast.26), calls=%async_computation.1 | async-start | bytes 6291456 | tf_op jit(solution)/shard_map/all_to_all | solution.py:315
  1385.3 315.0 %copy-start.1 = (bf16[2048,768]{1,0:T(8,128)(2,1)S(1)}, bf16[2048,768]{1,0:T(8,128)(2,1)}, u32[]{:S(2)}) copy-start(bf16[2048,768]{1,0:T(8,128)(2,1)} %param.19) | copy-start | bytes 9437188
  (128 other events, 649.9 us)
Sparse Core Ops, SparseCore 0:
  10.9 83.9 all-gather.5
  97.8 77.8 all-gather.9
  178.6 57.9 all-gather.7
  239.4 62.5 all-gather.11
  304.7 61.9 all-gather.13
  1033.3 99.6 reduce-scatter.7
  1139.3 148.1 reduce-scatter.9
  1293.7 123.4 reduce-scatter.5
  1423.7 135.1 reduce-scatter.13
  1565.2 135.0 reduce-scatter.11
where the time goes:
time: 1720 us; the launch traced here: 1710 us
  matrix products  641 us (37%)
  waiting for transfers between devices  468 us (27%)
  local copies, waits for them, and re-layouts  246 us (14%)
  blocking collectives  194 us (11%)
  other arithmetic  119 us (7%)
  starting transfers between devices  22.2 us (1%)
    reduce_scatter x5, waiting for transfers between devices, per_device(): lax.psum_scatter(grad_sums, ('dp', 'fsdp'), scatter_dimension=0, tiled=True)  311 us
    unnamed x2, blocking collectives  194 us
    dot_general x48, matrix products, head_scores(): lax.dot_general(query_head, key_head, cols_contract, preferred_element_ty...  137 us
    all_to_all x1, waiting for transfers between devices, per_device(): lax.all_to_all(send_x, ('dp', 'fsdp'), split_axis=0, concat_axis=0, tiled...  83.5 us
    unnamed x262, local copies, waits for them, and re-layouts  82.6 us
    all_to_all x1, waiting for transfers between devices, per_device(): lax.all_to_all(back_dx, ('dp', 'fsdp'), split_axis=0, concat_axis=0, tile...  70.7 us
    dot_general x24, matrix products, attend_back(): lax.dot_general(probs_low, dout_head, rows_contract, preferred_element_ty...  58.8 us
    dot_general x24, matrix products, attend_back(): lax.dot_general(dscores_low, query_head, rows_contract, preferred_element...  58.4 us
  transfers between devices with their start and end apart: 14, of which 5 were waited for; matrix products, arithmetic and copies ran while one was open for 31% of the time, Pallas kernels for 0%

commit v1 on v0

v1 whole, which is shorter than its diff:
```python
import functools
import math

import jax
import jax.numpy as jnp
from jax import lax
from jax.experimental import pallas as pl
from jax.experimental.pallas import tpu as pltpu
from jax.sharding import PartitionSpec as P

D = 768
HEADS = 12
HEAD = 64
FF = 3072
BIN = 1024
MB = 2
SLOTS = 2
PAGE = 16
LANES = 128
PAIRS = HEADS // 2
ROWS = MB * BIN
CHUNK = 768
PIECE = 256
BLOCK = 256
VMEM_LIMIT = 60 << 20

eps = 1e-05
neg_big = -1e30
AXES = ("dp", "fsdp")
f32 = jnp.float32
bf16 = jnp.bfloat16

NN = (((1,), (0,)), ((), ()))
NT = (((1,), (1,)), ((), ()))
TN = (((0,), (0,)), ((), ()))


def mm(a, b, dims):
    return lax.dot_general(a, b, dims, preferred_element_type=f32)


def params(*semantics):
    return pltpu.CompilerParams(dimension_semantics=semantics, vmem_limit_bytes=VMEM_LIMIT)


def fixed(shape):
    return pl.BlockSpec(shape, lambda *g: (0,) * len(shape), pipeline_mode=pl.Buffered(1))


def normalise(values):
    center = jnp.mean(values, axis=-1, keepdims=True)
    shifted = values - center
    spread = jnp.mean(shifted * shifted, axis=-1, keepdims=True)
    inv = lax.rsqrt(spread + eps)
    return shifted * inv, inv


def partner(tile):
    lane = lax.broadcasted_iota(jnp.int32, tile.shape, 1)
    ahead = pltpu.roll(tile, LANES - HEAD // 2, 1)
    behind = pltpu.roll(tile, HEAD // 2, 1)
    return jnp.where(lane % HEAD < HEAD // 2, ahead, behind)


def qkv_body(x_ref, gain_ref, w_ref, cos_ref, sin_ref, qkv_ref, a1_ref):
    xhat, _ = normalise(x_ref[...].astype(f32))
    a1 = (xhat * gain_ref[0:1, :]).astype(bf16)
    a1_ref[...] = a1
    cosine, sine = cos_ref[...], sin_ref[...]
    for part in range(3):
        u = mm(a1, w_ref[:, part * D : (part + 1) * D], NN)
        for t in range(D // LANES):
            tile = u[:, t * LANES : (t + 1) * LANES]
            if part < 2:
                tile = tile * cosine + partner(tile) * sine
            if part == 0:
                tile = tile * 0.125
            at = part * D + t * LANES
            qkv_ref[:, at : at + LANES] = tile.astype(bf16)


def qkv_call(x, gain, w, cosine, sine):
    rows = x.shape[0]
    blk = 256
    return pl.pallas_call(
        qkv_body,
        name="qkv",
        grid=(rows // blk,),
        in_specs=[
            pl.BlockSpec((blk, D), lambda i: (i, 0)),
            fixed((8, D)),
            fixed((D, 3 * D)),
            pl.BlockSpec((blk, LANES), lambda i: (i, 0)),
            pl.BlockSpec((blk, LANES), lambda i: (i, 0)),
        ],
        out_specs=[
            pl.BlockSpec((blk, 3 * D), lambda i: (i, 0)),
            pl.BlockSpec((blk, D), lambda i: (i, 0)),
        ],
        out_shape=[
            jax.ShapeDtypeStruct((rows, 3 * D), bf16),
            jax.ShapeDtypeStruct((rows, D), bf16),
        ],
        compiler_params=params("arbitrary"),
        cost_estimate=pl.CostEstimate(
            flops=2 * rows * D * 3 * D, bytes_accessed=rows * D * 10, transcendentals=0
        ),
    )(x, gain, w, cosine, sine)


def attend_body(q_ref, k_ref, v_ref, qa_ref, ka_ref, p_ref, o_ref, rl_ref):
    pair = pl.program_id(1)
    blk = 256

    @pl.when(pair == 0)
    def _():
        rl_ref[...] = jnp.zeros_like(rl_ref)

    keys = jnp.concatenate([k_ref[...], ka_ref[...]], axis=1)
    vals = jnp.concatenate([v_ref[...], jnp.ones((BIN, LANES), bf16)], axis=1)
    lane = lax.broadcasted_iota(jnp.int32, (blk, LANES), 1)
    for rb in range(BIN // blk):
        rows = pl.ds(rb * blk, blk)
        q = q_ref[rows, :]
        outs = []
        for h in range(2):
            mine = (lane >= HEAD) == (h == 1)
            qh = jnp.concatenate([jnp.where(mine, q, jnp.zeros_like(q)), qa_ref[rows, :]], axis=1)
            s = mm(qh, keys, NT)
            top = jnp.max(s, axis=1, keepdims=True)
            p = jnp.exp(s - top).astype(bf16)
            p_ref[0, h, rows, :] = p
            ol = mm(p, vals, NN)
            rl = 1.0 / ol[:, LANES:]
            outs.append(ol[:, :LANES] * rl)
            rl_ref[rows, :] = jnp.where(lane == 2 * pair + h, rl, rl_ref[rows, :])
        o_ref[rows, :] = jnp.where(lane < HEAD, outs[0], outs[1]).astype(bf16)


def attend_call(qkv, qa, ka):
    bins = qkv.shape[0] // BIN
    tile = (BIN, LANES)
    return pl.pallas_call(
        attend_body,
        name="attend",
        grid=(bins, PAIRS),
        in_specs=[
            pl.BlockSpec(tile, lambda b, p: (b, p)),
            pl.BlockSpec(tile, lambda b, p: (b, PAIRS + p)),
            pl.BlockSpec(tile, lambda b, p: (b, 2 * PAIRS + p)),
            pl.BlockSpec(tile, lambda b, p: (b, 0)),
            pl.BlockSpec(tile, lambda b, p: (b, 0)),
        ],
        out_specs=[
            pl.BlockSpec((1, 2, BIN, BIN), lambda b, p: (b, p, 0, 0)),
            pl.BlockSpec(tile, lambda b, p: (b, p)),
            pl.BlockSpec(tile, lambda b, p: (b, 0)),
        ],
        out_shape=[
            jax.ShapeDtypeStruct((bins, HEADS, BIN, BIN), bf16),
            jax.ShapeDtypeStruct((bins * BIN, D), bf16),
            jax.ShapeDtypeStruct((bins * BIN, LANES), f32),
        ],
        compiler_params=params("arbitrary", "arbitrary"),
        cost_estimate=pl.CostEstimate(
            flops=bins * HEADS * BIN * BIN * 1024,
            bytes_accessed=bins * HEADS * BIN * BIN * 2,
            transcendentals=bins * HEADS * BIN * BIN,
        ),
    )(qkv, qkv, qkv, qa, ka)


def attend_back_body(
    q_ref, k_ref, v_ref, do_ref, o_ref, rl_ref, p_ref, cos_ref, sin_ref, dq_ref, dk_ref, dv_ref,
    dq_acc, dkt_acc, dvt_acc,
):
    pair = pl.program_id(1)
    blk = 256
    lane = lax.broadcasted_iota(jnp.int32, (blk, LANES), 1)
    lane_full = lax.broadcasted_iota(jnp.int32, (BIN, LANES), 1)

    def head(h, carry):
        vals = jnp.concatenate([v_ref[...], jnp.where(lane_full < 3, 1.0, 0.0).astype(bf16)], axis=1)
        mine = (lane >= HEAD) == (h == 1)
        dkt = jnp.zeros((LANES, BIN), f32)
        dvt = jnp.zeros((LANES, BIN), f32)
        for rb in range(BIN // blk):
            rows = pl.ds(rb * blk, blk)
            rl = jnp.sum(jnp.where(lane == 2 * pair + h, rl_ref[rows, :], 0.0), axis=1, keepdims=True)
            do = jnp.where(mine, do_ref[rows, :].astype(f32) * rl, 0.0).astype(bf16)
            delta = jnp.sum(do.astype(f32) * o_ref[rows, :].astype(f32), axis=1, keepdims=True)
            high = delta.astype(bf16).astype(f32)
            rest = delta - high
            mid = rest.astype(bf16).astype(f32)
            extra = jnp.where(lane == 0, -high, jnp.where(lane == 1, -mid, jnp.where(lane == 2, mid - rest, 0.0)))
            dp = mm(jnp.concatenate([do, extra.astype(bf16)], axis=1), vals, NT)
            p = p_ref[0, h, rows, :]
            ds = (p.astype(f32) * dp).astype(bf16)
            dq_acc[h, rows, :] = mm(ds, k_ref[...], NN)
            dkt += mm(q_ref[rows, :], ds, TN)
            dvt += mm(do, p, TN)
        dkt_acc[h] = dkt
        dvt_acc[h] = dvt
        return carry

    lax.fori_loop(0, 2, head, 0)
    sub = lax.broadcasted_iota(jnp.int32, (LANES, BIN), 0)
    dk = jnp.where(sub < HEAD, dkt_acc[0], dkt_acc[1]).T
    dv = jnp.where(sub < HEAD, dvt_acc[0], dvt_acc[1]).T
    cosine, sine = cos_ref[...], sin_ref[...]
    dq = jnp.where(lane_full < HEAD, dq_acc[0], dq_acc[1]) * 0.125
    dq_ref[...] = (dq * cosine - partner(dq) * sine).astype(bf16)
    dk_ref[...] = (dk * cosine - partner(dk) * sine).astype(bf16)
    dv_ref[...] = dv.astype(bf16)


def attend_back_call(qkv, do, o, rl, p, cosine, sine):
    bins = qkv.shape[0] // BIN
    tile = (BIN, LANES)
    grad = jax.ShapeDtypeStruct((bins * BIN, D), bf16)
    by_pair = pl.BlockSpec(tile, lambda b, p: (b, p))
    by_bin = pl.BlockSpec(tile, lambda b, p: (b, 0))
    return pl.pallas_call(
        attend_back_body,
        name="attend_back",
        grid=(bins, PAIRS),
        in_specs=[
            by_pair,
            pl.BlockSpec(tile, lambda b, p: (b, PAIRS + p)),
            pl.BlockSpec(tile, lambda b, p: (b, 2 * PAIRS + p)),
            by_pair,
            by_pair,
            by_bin,
            pl.BlockSpec((1, 2, BIN, BIN), lambda b, p: (b, p, 0, 0)),
            by_bin,
            by_bin,
        ],
        out_specs=[by_pair, by_pair, by_pair],
        out_shape=[grad, grad, grad],
        scratch_shapes=[
            pltpu.VMEM((2, BIN, LANES), f32),
            pltpu.VMEM((2, LANES, BIN), f32),
            pltpu.VMEM((2, LANES, BIN), f32),
        ],
        compiler_params=params("arbitrary", "arbitrary"),
        cost_estimate=pl.CostEstimate(
            flops=bins * HEADS * BIN * BIN * 2048,
            bytes_accessed=bins * HEADS * BIN * BIN * 2,
            transcendentals=0,
        ),
    )(qkv, qkv, qkv, do, o, rl, p, cosine, sine)


def rows_body(
    spans_ref, x_ref, o_ref, dy_ref, ada_ref, wo_ref, wu_ref, wd_ref,
    y_ref, dx1_ref, do_ref, dada_ref, go_hbm, gu_hbm, gd_hbm,
    go_acc, gu_acc, gd_acc, hb_ref, dmlp_ref, mlp_ref, dh_ref, stage_ref, sem,
):
    step = pl.program_id(0)
    last = pl.num_programs(0) - 1
    here = step // (BIN // BLOCK)
    first_row = (step % (BIN // BLOCK)) * BLOCK

    @pl.when(step == 0)
    def _():
        go_acc[...] = jnp.zeros_like(go_acc)
        gu_acc[...] = jnp.zeros_like(gu_acc)
        gd_acc[...] = jnp.zeros_like(gd_acc)
        dada_ref[...] = jnp.zeros_like(dada_ref)

    row = lax.broadcasted_iota(jnp.int32, (BLOCK, 1), 0) + first_row
    owned = []
    for k in range(SLOTS):
        start = spans_ref[here * SLOTS + k, 0]
        length = spans_ref[here * SLOTS + k, 1]
        owned.append(jnp.where((row >= start) & (row < start + length), 1.0, 0.0).astype(f32))
    live = owned[0] + owned[1]

    def ada(part):
        cols = slice(part * D, (part + 1) * D)
        return sum(owned[k] * ada_ref[pl.ds(here * SLOTS + k, 1), cols] for k in range(SLOTS))

    def add_slots(part, values):
        cols = slice(part * D, (part + 1) * D)
        for k in range(SLOTS):
            at = pl.ds(here * SLOTS + k, 1)
            dada_ref[at, cols] += jnp.sum(owned[k] * values, axis=0, keepdims=True)

    o = o_ref[...]
    x1 = x_ref[...].astype(f32) + mm(o, wo_ref[...], NN)
    xhat, inv = normalise(x1)
    one_scale = 1.0 + ada(0)
    hb_ref[...] = (xhat * one_scale + ada(1)).astype(bf16)
    gate = ada(2)
    dy = live * dy_ref[...].astype(f32)
    dmlp_ref[...] = (dy * gate).astype(bf16)
    mlp_ref[...] = jnp.zeros_like(mlp_ref)
    dh_ref[...] = jnp.zeros_like(dh_ref)
    c0 = math.sqrt(2.0 / math.pi)

    def chunk(c, carry):
        cols = pl.ds(pl.multiple_of(c * CHUNK, CHUNK), CHUNK)
        u = mm(hb_ref[...], wu_ref[:, cols], NN)
        uu = u * u
        t = jnp.tanh(u * (c0 + (c0 * 0.044715) * uu))
        half = 0.5 + 0.5 * t
        gb = (u * half).astype(bf16)
        mlp_ref[...] += mm(gb, wd_ref[cols, :], NN)
        gd_acc[cols, :] += mm(gb, dmlp_ref[...], TN)
        slope = half + (u * (1.0 - t * t)) * (0.5 * c0 + (1.5 * c0 * 0.044715) * uu)
        du = (mm(dmlp_ref[...], wd_ref[cols, :], NT) * slope).astype(bf16)
        dh_ref[...] += mm(du, wu_ref[:, cols], NT)
        gu_acc[:, cols] += mm(hb_ref[...], du, TN)
        return carry

    lax.fori_loop(0, FF // CHUNK, chunk, 0)
    mlp, dh = mlp_ref[...], dh_ref[...]
    y_ref[...] = (live * (x1 + gate * mlp)).astype(bf16)
    add_slots(2, dy * mlp)
    add_slots(1, dh)
    add_slots(0, dh * xhat)
    e = dh * one_scale
    dx1 = dy + (e - jnp.mean(e, axis=1, keepdims=True) - xhat * jnp.mean(e * xhat, axis=1, keepdims=True)) * inv
    dx1_ref[...] = dx1
    dattn = dx1.astype(bf16)
    go_acc[...] += mm(o, dattn, TN)
    do_ref[...] = mm(dattn, wo_ref[...], NT).astype(bf16)

    @pl.when(step == last)
    def _():
        pieces = []
        for acc, out in ((go_acc, go_hbm), (gu_acc, gu_hbm), (gd_acc, gd_hbm)):
            for r in range(0, acc.shape[0], PIECE):
                for c in range(0, acc.shape[1], D):
                    at = (slice(r, r + PIECE), slice(c, c + D))
                    pieces.append((acc.at[at], out.at[at]))
        copies = [None, None]
        for i, (acc, out) in enumerate(pieces):
            slot = i % 2
            if copies[slot] is not None:
                copies[slot].wait()
            stage_ref[slot] = acc[...].astype(bf16)
            copies[slot] = pltpu.make_async_copy(stage_ref.at[slot], out, sem.at[slot])
            copies[slot].start()
        for copy in copies:
            copy.wait()


def rows_call(spans, x, o, dy, ada, w_out, w_up, w_down):
    rows = x.shape[0]
    block = pl.BlockSpec((BLOCK, D), lambda i, s: (i, 0))
    anywhere = pl.BlockSpec(memory_space=pl.ANY)
    return pl.pallas_call(
        rows_body,
        name="rows",
        grid_spec=pltpu.PrefetchScalarGridSpec(
            num_scalar_prefetch=1,
            grid=(rows // BLOCK,),
            in_specs=[
                block, block, block, fixed((8, 3 * D)), fixed((D, D)), fixed((D, FF)), fixed((FF, D)),
            ],
            out_specs=[
                block, block, block, pl.BlockSpec((8, 3 * D), lambda i, s: (0, 0)), anywhere, anywhere, anywhere,
            ],
            scratch_shapes=[
                pltpu.VMEM((D, D), f32),
                pltpu.VMEM((D, FF), f32),
                pltpu.VMEM((FF, D), f32),
                pltpu.VMEM((BLOCK, D), bf16),
                pltpu.VMEM((BLOCK, D), bf16),
                pltpu.VMEM((BLOCK, D), f32),
                pltpu.VMEM((BLOCK, D), f32),
                pltpu.VMEM((2, PIECE, D), bf16),
                pltpu.SemaphoreType.DMA((2,)),
            ],
        ),
        out_shape=[
            jax.ShapeDtypeStruct((rows, D), bf16),
            jax.ShapeDtypeStruct((rows, D), f32),
            jax.ShapeDtypeStruct((rows, D), bf16),
            jax.ShapeDtypeStruct((8, 3 * D), f32),
            jax.ShapeDtypeStruct((D, D), bf16),
            jax.ShapeDtypeStruct((D, FF), bf16),
            jax.ShapeDtypeStruct((FF, D), bf16),
        ],
        compiler_params=params("arbitrary"),
        cost_estimate=pl.CostEstimate(
            flops=6 * rows * D * (D + 2 * FF), bytes_accessed=rows * D * 14, transcendentals=rows * FF
        ),
    )(spans, x, o, dy, ada, w_out, w_up, w_down)


def qkv_back_body(x_ref, dx1_ref, dq_ref, dk_ref, dv_ref, gain_ref, w_ref, dx_ref, gg_ref):
    @pl.when(pl.program_id(0) == 0)
    def _():
        gg_ref[...] = jnp.zeros_like(gg_ref)

    xhat, inv = normalise(x_ref[...].astype(f32))
    dn = mm(dq_ref[...], w_ref[:, :D], NT)
    dn += mm(dk_ref[...], w_ref[:, D : 2 * D], NT)
    dn += mm(dv_ref[...], w_ref[:, 2 * D :], NT)
    gg_ref[0:1, :] += jnp.sum(dn * xhat, axis=0, keepdims=True)
    e = dn * gain_ref[0:1, :]
    back = (e - jnp.mean(e, axis=1, keepdims=True) - xhat * jnp.mean(e * xhat, axis=1, keepdims=True)) * inv
    dx_ref[...] = (dx1_ref[...] + back).astype(bf16)


def qkv_back_call(x, dx1, dq, dk, dv, gain, w):
    rows = x.shape[0]
    blk = 256
    block = pl.BlockSpec((blk, D), lambda i: (i, 0))
    return pl.pallas_call(
        qkv_back_body,
        name="qkv_back",
        grid=(rows // blk,),
        in_specs=[block, block, block, block, block, fixed((8, D)), fixed((D, 3 * D))],
        out_specs=[block, pl.BlockSpec((8, D), lambda i: (0, 0))],
        out_shape=[jax.ShapeDtypeStruct((rows, D), bf16), jax.ShapeDtypeStruct((8, D), f32)],
        compiler_params=params("arbitrary"),
        cost_estimate=pl.CostEstimate(
            flops=2 * rows * D * 3 * D, bytes_accessed=rows * D * 14, transcendentals=0
        ),
    )(x, dx1, dq, dk, dv, gain, w)


def qkv_grad_body(a1_ref, dq_ref, dk_ref, dv_ref, out_ref, acc_ref):
    step = pl.program_id(0)

    @pl.when(step == 0)
    def _():
        acc_ref[...] = jnp.zeros_like(acc_ref)

    a1 = a1_ref[...]
    for part, ref in enumerate((dq_ref, dk_ref, dv_ref)):
        acc_ref[:, part * D : (part + 1) * D] += mm(a1, ref[...], TN)

    @pl.when(step == pl.num_programs(0) - 1)
    def _():
        out_ref[...] = acc_ref[...].astype(bf16)


def qkv_grad_call(a1, dq, dk, dv):
    rows = a1.shape[0]
    blk = 512
    block = pl.BlockSpec((blk, D), lambda i: (i, 0))
    return pl.pallas_call(
        qkv_grad_body,
        name="qkv_grad",
        grid=(rows // blk,),
        in_specs=[block, block, block, block],
        out_specs=pl.BlockSpec((D, 3 * D), lambda i: (0, 0)),
        out_shape=jax.ShapeDtypeStruct((D, 3 * D), bf16),
        scratch_shapes=[pltpu.VMEM((D, 3 * D), f32)],
        compiler_params=params("arbitrary"),
        cost_estimate=pl.CostEstimate(
            flops=2 * rows * D * 3 * D, bytes_accessed=rows * D * 8, transcendentals=0
        ),
    )(a1, dq, dk, dv)


def feature_angles(time_steps, width):
    half = width // 2
    frequency = jnp.exp(jnp.arange(half, dtype=f32) * (-math.log(10000.0) / half))
    return time_steps.astype(f32)[:, None] * frequency[None, :]


def time_features(time_steps, width):
    angles = feature_angles(time_steps, width)
    return jnp.concatenate([jnp.cos(angles), jnp.sin(angles)], axis=-1).astype(bf16)


def row_tables(seq_spans):
    row = jnp.arange(BIN, dtype=jnp.int32)[None, :, None]
    spans = seq_spans.reshape(MB, 1, SLOTS, 2)
    offset = row - spans[..., 0]
    member = (offset >= 0) & (offset < spans[..., 1])
    position = jnp.sum(jnp.where(member, offset, 0), axis=2).astype(f32).reshape(ROWS, 1)
    lane = jnp.arange(LANES, dtype=jnp.int32)[None, :]
    half = HEAD // 2
    frequency = jnp.exp((lane % half).astype(f32) * (-math.log(10000.0) / half))
    angle = position * frequency
    cosine = jnp.cos(angle)
    sine = jnp.sin(angle) * jnp.where(lane % HEAD < half, -1.0, 1.0)
    member = member.reshape(ROWS, SLOTS)
    slot = jnp.arange(LANES, dtype=jnp.int32)[None, :]
    mine = jnp.sum(jnp.where((slot[:, None, :] == jnp.arange(SLOTS)[None, :, None]), member[:, :, None], False), axis=1)
    query_mask = jnp.where(mine > 0, neg_big, 0.0).astype(bf16)
    key_mask = jnp.where((mine == 0) & (slot < SLOTS), 1.0, 0.0).astype(bf16)
    return cosine, sine, query_mask, key_mask


def page_plan(page_deal, pages_dev, shards, device):
    per_peer = pages_dev // shards
    ids = jnp.arange(pages_dev, dtype=jnp.int32)
    deal = lax.dynamic_slice_in_dim(page_deal, device * pages_dev, pages_dev)
    target = deal // pages_dev
    earlier = (target[:, None] == target[None, :]) & (deal[None, :] < deal[:, None])
    send_pos = target * per_peer + jnp.sum(earlier.astype(jnp.int32), axis=1)
    send_order = jnp.sum(jnp.where(send_pos[None, :] == ids[:, None], ids[None, :], 0), axis=1)
    all_ids = jnp.arange(page_deal.shape[0], dtype=jnp.int32)
    hit = page_deal[None, :] == (device * pages_dev + ids)[:, None]
    owned = jnp.sum(jnp.where(hit, all_ids[None, :], 0), axis=1)
    source = owned // pages_dev
    before = (source[:, None] == source[None, :]) & (ids[None, :] < ids[:, None])
    recv_pos = source * per_peer + jnp.sum(before.astype(jnp.int32), axis=1)
    recv_order = jnp.sum(jnp.where(recv_pos[None, :] == ids[:, None], ids[None, :], 0), axis=1)
    return send_pos, send_order, recv_pos, recv_order


def pages(values):
    return values.reshape(-1, PAGE, D)


def exchange(values, shards):
    sent = values.reshape(shards, -1, PAGE, D)
    got = lax.all_to_all(sent, AXES, split_axis=0, concat_axis=0, tiled=True)
    return got.reshape(-1, PAGE, D)


def per_device(
    x_given, cotangent, norm_gain, w_qkv, w_out, w_ada, w_up, w_down, seq_spans, time_steps, page_deal
):
    shards = lax.axis_size(AXES)
    device = lax.axis_index(AXES)
    rows_dev = x_given.shape[0]
    pages_dev = rows_dev // PAGE
    send_pos, send_order, recv_pos, recv_order = page_plan(page_deal, pages_dev, shards, device)
    x = exchange(pages(x_given)[send_order], shards)[recv_pos].reshape(rows_dev, D)
    dy = exchange(pages(cotangent)[send_order], shards)[recv_pos].reshape(rows_dev, D)

    def gather(w):
        return lax.all_gather(w, AXES, axis=0, tiled=True)

    qkv_all = gather(w_qkv)
    ada_ext = jnp.concatenate([w_ada, jnp.broadcast_to(norm_gain[:, None], (norm_gain.shape[0], LANES))], axis=1)
    ada_ext = gather(ada_ext)
    out_all, up_all, down_all = gather(w_out), gather(w_up), gather(w_down)
    ada_all = ada_ext[:, : 3 * D]
    gain = jnp.broadcast_to(ada_ext[:, 3 * D].astype(f32)[None, :], (8, D))

    cosine, sine, query_mask, key_mask = row_tables(seq_spans)
    time_feat = time_features(time_steps, D)
    ada_seq = jnp.dot(time_feat, ada_all, preferred_element_type=f32)
    ada_seq = jnp.concatenate([ada_seq, jnp.zeros_like(ada_seq)], axis=0)

    qkv, a1 = qkv_call(x, gain, qkv_all, cosine, sine)
    p, o, rl = attend_call(qkv, query_mask, key_mask)
    y, dx1, do, dada, go, gu, gd = rows_call(seq_spans, x, o, dy, ada_seq, out_all, up_all, down_all)

    output = exchange(pages(y)[recv_order], shards)[send_pos].reshape(rows_dev, D)

    def reduce(g):
        return lax.psum_scatter(g, AXES, scatter_dimension=0, tiled=True)

    up_grad, down_grad, out_grad = reduce(gu), reduce(gd), reduce(go)
    slots = time_steps.shape[0]
    steps_col = jnp.broadcast_to(time_steps.astype(f32)[:, None], (slots, LANES))
    slot_rows = jnp.concatenate([dada[:slots], steps_col], axis=1)
    slot_all = lax.all_gather(slot_rows, AXES, axis=0, tiled=True)
    own = norm_gain.shape[0]
    half = D // 2
    feature = device * own + jnp.arange(own, dtype=jnp.int32)
    frequency = jnp.exp((feature % half).astype(f32) * (-math.log(10000.0) / half))
    angle = slot_all[:, 3 * D : 3 * D + 1] * frequency[None, :]
    feat_own = jnp.where(feature[None, :] < half, jnp.cos(angle), jnp.sin(angle)).astype(bf16).astype(f32)
    ada_grad = lax.dot_general(feat_own, slot_all[:, : 3 * D], TN, precision=lax.Precision.HIGHEST)

    dq, dk, dv = attend_back_call(qkv, do, o, rl, p, cosine, sine)
    dx, gg = qkv_back_call(x, dx1, dq, dk, dv, gain, qkv_all)
    input_grad = exchange(pages(dx)[recv_order], shards)[send_pos].reshape(rows_dev, D)
    gq = qkv_grad_call(a1, dq, dk, dv)
    gq = jnp.concatenate([gq, jnp.broadcast_to(gg[0].astype(bf16)[:, None], (D, LANES))], axis=1)
    gq = reduce(gq)
    return (
        output,
        input_grad,
        gq[:, 3 * D].astype(f32),
        gq[:, : 3 * D].astype(f32),
        out_grad.astype(f32),
        ada_grad,
        up_grad.astype(f32),
        down_grad.astype(f32),
    )


def solution(mesh):
    placed = P(AXES, None)
    vector = P(AXES)
    return jax.shard_map(
        per_device,
        mesh=mesh,
        in_specs=(placed, placed, vector, placed, placed, placed, placed, placed, placed, vector, P()),
        out_specs=(placed, placed, vector, placed, placed, placed, placed, placed),
        check_vma=False,
    )
```

time: 1720 us -> 1080 us (0.63)
  matrix products: 641 us -> 5.37 us
  Pallas kernels: 0 us -> 270 us
  waiting for transfers between devices: 468 us -> 708 us
  local copies, waits for them, and re-layouts: 246 us -> 36 us
  blocking collectives: 194 us -> 0 us
  other arithmetic: 119 us -> 26.1 us
    dot_general x198 -> x2, matrix products: 641 us -> 5.37 us  [the longest x1 2.78 us: per_device(): lax.dot_general(feat_own, slot_all[:, :3 * D], TN, precision=lax.Precisio...]
    pallas_call x0 -> x6, Pallas kernels: none -> 270 us  [the longest x1 119 us: rows_call(): pl.pallas_call(rows_body, name='rows', grid_spec=pltpu.PrefetchScalarGrid...]
    unnamed x2 -> x0, blocking collectives: 194 us -> none
    all_gather x5 -> x6, waiting for transfers between devices: 0.05 us -> 156 us  [the longest x5 102 us: gather(): return lax.all_gather(w, AXES, axis=0, tiled=True)]
    reduce_scatter x5 -> x3, waiting for transfers between devices: 311 us -> 209 us  [reduce(): return lax.psum_scatter(g, AXES, scatter_dimension=0, tiled=True)]
    unnamed x10 -> x11, waiting for transfers between devices: 3.2 us -> 101 us
    all_to_all x4, waiting for transfers between devices: 154 us -> 242 us  [exchange(): got = lax.all_to_all(sent, AXES, split_axis=0, concat_axis=0, tiled=True)]
    unnamed x262 -> x34, local copies, waits for them, and re-layouts: 82.6 us -> 4.72 us
  transfers between devices with their start and end apart: 14 -> 14, of which waited for: 5 -> 9; matrix products, arithmetic and copies ran while one was open for 31% -> 6% of each run, Pallas kernels for 0% -> 14%
where the time goes in v1:
time: 1080 us
  waiting for transfers between devices  708 us (66%)
  Pallas kernels  270 us (25%)
  local copies, waits for them, and re-layouts  36 us (3%)
  other arithmetic  26.1 us (2%)
  starting transfers between devices  18 us (2%)
  between operations  14.5 us (1%)
    all_to_all x4, waiting for transfers between devices, exchange(): got = lax.all_to_all(sent, AXES, split_axis=0, concat_axis=0, tiled=True)  242 us
    reduce_scatter x3, waiting for transfers between devices, reduce(): return lax.psum_scatter(g, AXES, scatter_dimension=0, tiled=True)  209 us
    pallas_call x1, Pallas kernels, rows_call(): pl.pallas_call(rows_body, name='rows', grid_spec=pltpu.PrefetchScalarGrid...  119 us
    all_gather x5, waiting for transfers between devices, gather(): return lax.all_gather(w, AXES, axis=0, tiled=True)  102 us
    unnamed x11, waiting for transfers between devices  101 us
    pallas_call x1, Pallas kernels, attend_back_call(): pl.pallas_call(attend_back_body, name='attend_back', grid=(bins, PAIRS),...  65.9 us
    all_gather x1, waiting for transfers between devices, per_device(): slot_all = lax.all_gather(slot_rows, AXES, axis=0, tiled=True)  53.8 us
    pallas_call x1, Pallas kernels, attend_call(): pl.pallas_call(attend_body, name='attend', grid=(bins, PAIRS), in_specs=[...  40.9 us
  transfers between devices with their start and end apart: 14, of which 9 were waited for; matrix products, arithmetic and copies ran while one was open for 6% of the time, Pallas kernels for 14%

profile of v1, /device:TPU:0, one launch (start us, length us, event | category | flops | bytes accessed | tf_op | source)
XLA Modules:
  0.0 1077.6 jit_solution(11998233769766942892)
XLA Ops:
  13.4 2.4 gather_fusion
  15.8 7.3 all-to-all-start
  23.1 4.3 gather_fusion.2
  27.5 84.3 %all-to-all-done = bf16[32,4,16,768]{3,2,1,0:T(8,128)(2,1)S(1)} async-done(((bf16[32,4,16,768]{3,2,1,0:T(8,128)(2,1)}), bf16[32,4,16,768]{3,2,1,0:T(8,128)(2,1)S(1)}, u32[]{:S(2)}, u32[]{:S(2)}) %all-to-all-start) | async-done | bytes 3145760 | tf_op jit(solution)/shard_map/all_to_all | solution.py:516
  111.8 3.7 all-to-all-start.1
  121.4 5.6 fusion.4
  127.0 2.4 gather_fusion.1
  129.4 72.3 %all-to-all-done.1 = bf16[32,4,16,768]{3,2,1,0:T(8,128)(2,1)} async-done(((bf16[32,4,16,768]{3,2,1,0:T(8,128)(2,1)}), bf16[32,4,16,768]{3,2,1,0:T(8,128)(2,1)}, u32[]{:S(2)}, u32[]{:S(2)}) %all-to-all-start.1) | async-done | bytes 3145760 | tf_op jit(solution)/shard_map/all_to_all | solution.py:516
  201.7 4.3 gather_fusion.3
  206.0 2.6 fusion
  211.0 15.1 %qkv.1 = (bf16[2048,2304]{1,0:T(8,128)(2,1)}, bf16[2048,768]{1,0:T(8,128)(2,1)}) custom-call(bf16[2048,768]{1,0:T(8,128)(2,1)} %bitcast.70, f32[8,768]{1,0:T(8,128)} %broadcast_in_dim.148.gain_ref, bf16[768,2304]{1,0:T(8,128)(2,1)} %all-gather.10.cloned.1.call-done.w_ref, f32[2048,128]{1,0:T(8,128)} %get-tuple-element.49.cos_ref, ...), custom_call_target="tpu_custom_call" | custom-call | flops 7247757312 | bytes 15728640 | tf_op jit(solution)/shard_map/qkv/pallas_call | solution.py:85
  226.1 40.9 %attend.1 = (bf16[2,12,1024,1024]{3,2,1,0:T(8,128)(2,1)}, bf16[2048,768]{1,0:T(8,128)(2,1)}, f32[2048,128]{1,0:T(8,128)}) custom-call(bf16[2048,2304]{1,0:T(8,128)(2,1)} %get-tuple-element.25.q_ref.k_ref.v_ref, bf16[2048,2304]{1,0:T(8,128)(2,1)} %get-tuple-element.25.q_ref.k_ref.v_ref, bf16[2048,2304]{1,0:T(8,128)(2,1)} %get-tuple-element.25.q_ref.k_ref.v_ref, ...), custom_call_target="tpu_custom_call" | custom-call | flops 25769803776 | bytes 50331648 | tf_op jit(solution)/shard_map/attend/pallas_call | solution.py:143
  267.0 37.3 %all-gather.14.cloned.1.call-done.wu_ref = bf16[768,3072]{1,0:T(8,128)(2,1)} async-done(((bf16[24,3072]{1,0:T(8,128)(2,1)}), bf16[768,3072]{1,0:T(8,128)(2,1)}) %all-gather.14.cloned.1.call-update) | async-done | bytes 4718608 | tf_op jit(solution)/shard_map/all_gather | solution.py:532
  304.3 64.7 %all-gather.16.cloned.1.call-done.wd_ref = bf16[3072,768]{1,0:T(8,128)(2,1)} async-done(((bf16[96,768]{1,0:T(8,128)(2,1)}), bf16[3072,768]{1,0:T(8,128)(2,1)}) %all-gather.16.cloned.1.call-update) | async-done | bytes 4718608 | tf_op jit(solution)/shard_map/all_gather | solution.py:532
  369.0 118.7 %rows.1 = (bf16[2048,768]{1,0:T(8,128)(2,1)}, f32[2048,768]{1,0:T(8,128)}, bf16[2048,768]{1,0:T(8,128)(2,1)}, f32[8,2304]{1,0:T(8,128)}, bf16[768,768]{1,0:T(8,1...) custom-call(s32[4,2]{1,0:T(4,128)} %copy.25.spans_ref, bf16[2048,768]{1,0:T(8,128)(2,1)} %bitcast.71, ...), custom_call_target="tpu_custom_call" | custom-call | flops 65229815808 | bytes 22020096 | tf_op jit(solution)/shard_map/rows/pallas_call | solution.py:353
  487.8 65.9 %attend_back.1 = (bf16[2048,768]{1,0:T(8,128)(2,1)}, bf16[2048,768]{1,0:T(8,128)(2,1)}, bf16[2048,768]{1,0:T(8,128)(2,1)}) custom-call(bf16[2048,2304]{1,0:T(8,128)(2,1)} %get-tuple-element.25.q_ref.k_ref.v_ref, bf16[2048,2304]{1,0:T(8,128)(2,1)} %get-tuple-element.25.q_ref.k_ref.v_ref, bf16[2048,2304]{1,0:T(8,128)(2,1)} %get-tuple-element.25.q_ref.k_ref.v_ref, ...), custom_call_target="tpu_custom_call" | custom-call | flops 51539607552 | bytes 50331648 | tf_op jit(solution)/shard_map/attend_back/pallas_call | solution.py:223
  553.7 16.2 %qkv_back.1 = (bf16[2048,768]{1,0:T(8,128)(2,1)}, f32[8,768]{1,0:T(8,128)}) custom-call(bf16[2048,768]{1,0:T(8,128)(2,1)} %bitcast.72, f32[2048,768]{1,0:T(8,128)} %get-tuple-element.28.dx1_ref, bf16[2048,768]{1,0:T(8,128)(2,1)} %get-tuple-element.32.dq_ref, bf16[2048,768]{1,0:T(8,128)(2,1)} %get-tuple-element.33.dk_ref, ...), custom_call_target="tpu_custom_call" | custom-call | flops 7247757312 | bytes 22020096 | tf_op jit(solution)/shard_map/qkv_back/pallas_call | solution.py:412
  570.6 12.7 %qkv_grad.1 = bf16[768,2304]{1,0:T(8,128)(2,1)} custom-call(bf16[2048,768]{1,0:T(8,128)(2,1)} %get-tuple-element.36.a1_ref, bf16[2048,768]{1,0:T(8,128)(2,1)} %get-tuple-element.32.dq_ref, bf16[2048,768]{1,0:T(8,128)(2,1)} %get-tuple-element.33.dk_ref, bf16[2048,768]{1,0:T(8,128)(2,1)} %get-tuple-element.34.dv_ref), custom_call_target="tpu_custom_call" | custom-call | flops 7247757312 | bytes 12582912 | tf_op jit(solution)/shard_map/qkv_grad/pallas_call | solution.py:446
  583.5 4.1 pad_maximum_fusion
  590.1 2.4 gather_fusion.6
  592.5 3.0 all-to-all-start.3
  596.1 4.3 gather_fusion.4
  600.4 85.7 %all-to-all-done.3 = bf16[32,4,16,768]{3,2,1,0:T(8,128)(2,1)S(1)} async-done(((bf16[32,4,16,768]{3,2,1,0:T(8,128)(2,1)}), bf16[32,4,16,768]{3,2,1,0:T(8,128)(2,1)S(1)}, u32[]{:S(2)}, u32[]{:S(2)}) %all-to-all-start.3) | async-done | bytes 3145760 | tf_op jit(solution)/shard_map/all_to_all | solution.py:516
  686.2 3.7 all-to-all-start.2
  691.3 97.0 %all-reduce.4.cloned.1.call-done = bf16[768,2432]{1,0:T(8,128)(2,1)} async-done(((bf16[768,2432]{1,0:T(8,128)(2,1)}), bf16[768,2432]{1,0:T(8,128)(2,1)}) %all-reduce.4.cloned.1.call-update) | async-done | bytes 3735568
  791.3 53.8 %all-gather.18.cloned.1.call-done = f32[32,4,2432]{2,1,0:T(4,128)} async-done(((f32[1,4,2432]{2,1,0:T(4,128)}), f32[32,4,2432]{2,1,0:T(4,128)}) %all-gather.18.cloned.1.call-update) | async-done | bytes 1245200 | tf_op jit(solution)/shard_map/all_gather | solution.py:559
  845.1 2.6 reshape.418
  848.6 2.8 fusion.2
  851.4 2.4 gather_fusion.7
  853.8 4.5 gather_fusion.5
  858.4 98.9 %reduce-scatter.6.cloned.1.call-done = bf16[24,3072]{1,0:T(8,128)(2,1)} async-done(((bf16[768,3072]{1,0:T(8,128)(2,1)}), bf16[24,3072]{1,0:T(8,128)(2,1)}) %reduce-scatter.6.cloned.1.call-update) | async-done | bytes 147472 | tf_op jit(solution)/shard_map/reduce_scatter | solution.py:553
  958.9 110.2 %reduce-scatter.8.cloned.1.call-done = bf16[96,768]{1,0:T(8,128)(2,1)} async-done(((bf16[3072,768]{1,0:T(8,128)(2,1)}), bf16[96,768]{1,0:T(8,128)(2,1)}) %reduce-scatter.8.cloned.1.call-update) | async-done | bytes 147472 | tf_op jit(solution)/shard_map/reduce_scatter | solution.py:553
  (108 shorter events, 26.9 us)
Async XLA Ops:
  7.2 6.2 copy-start
  7.2 198.9 %all-gather.8.cloned.1.call-start = ((), (), s32[]{:S(2)}) async-start(), calls=%async_computation.7 | async-start | bytes 3852288 | tf_op jit(solution)/shard_map/all_gather | solution.py:532
  9.7 200.6 %all-gather.10.cloned.1.call-start = ((), (), s32[]{:S(2)}) async-start(), calls=%async_computation.8 | async-start | bytes 3649536 | tf_op jit(solution)/shard_map/all_gather | solution.py:532
  10.5 256.5 %all-gather.12.cloned.1.call-start = ((), (), s32[]{:S(2)}) async-start(), calls=%async_computation.9 | async-start | bytes 1216512 | tf_op jit(solution)/shard_map/all_gather | solution.py:532
  11.2 293.1 %all-gather.14.cloned.1.call-start = ((), (), s32[]{:S(2)}) async-start(), calls=%async_computation.10 | async-start | bytes 4866048 | tf_op jit(solution)/shard_map/all_gather | solution.py:532
  15.8 96.0 %all-to-all-start = ((bf16[32,4,16,768]{3,2,1,0:T(8,128)(2,1)}), bf16[32,4,16,768]{3,2,1,0:T(8,128)(2,1)S(1)}, u32[]{:S(2)}, u32[]{:S(2)}) async-start(bf16[32,4,16,768]{3,2,1,0:T(8,128)(2,1)} %bitcast.67), calls=%async_computation | async-start | bytes 6291456 | tf_op jit(solution)/shard_map/all_to_all | solution.py:516
  111.8 4.3 copy-start.5
  111.8 5.2 copy-start.11
  111.8 5.3 copy-start.4
  111.8 90.0 %all-to-all-start.1 = ((bf16[32,4,16,768]{3,2,1,0:T(8,128)(2,1)}), bf16[32,4,16,768]{3,2,1,0:T(8,128)(2,1)}, u32[]{:S(2)}, u32[]{:S(2)}) async-start(bf16[32,4,16,768]{3,2,1,0:T(8,128)(2,1)} %bitcast.63), calls=%async_computation.1 | async-start | bytes 6291456 | tf_op jit(solution)/shard_map/all_to_all | solution.py:516
  115.5 253.6 %all-gather.16.cloned.1.call-start = ((), (), s32[]{:S(2)}) async-start(), calls=%async_computation.11 | async-start | bytes 4866048 | tf_op jit(solution)/shard_map/all_gather | solution.py:532
  116.1 573.9 %reduce-scatter.4.cloned.1.call-start = ((), (), s32[]{:S(2)}) async-start(), calls=%async_computation.12 | async-start | bytes 1216512 | tf_op jit(solution)/shard_map/reduce_scatter | solution.py:553
  117.0 2.9 copy-start.6
  117.5 2.5 copy-start.9
  117.7 0.5 copy-start.12
  487.8 300.5 %all-reduce.4.cloned.1.call-start = ((), (), s32[]{:S(2)}) async-start(), calls=%async_computation.16 | async-start | bytes 7471104
  587.6 0.9 copy-start.3
  587.6 0.9 copy-start.7
  587.6 1.7 copy-start.10
  587.6 1.7 copy-start.13
  587.7 2.5 copy-start.2
  587.7 257.4 %all-gather.18.cloned.1.call-start = ((), (), s32[]{:S(2)}) async-start(), calls=%async_computation.15 | async-start | bytes 1284096 | tf_op jit(solution)/shard_map/all_gather | solution.py:559
  589.2 368.0 %reduce-scatter.6.cloned.1.call-start = ((), (), s32[]{:S(2)}) async-start(), calls=%async_computation.13 | async-start | bytes 4866048 | tf_op jit(solution)/shard_map/reduce_scatter | solution.py:553
  592.5 93.6 %all-to-all-start.3 = ((bf16[32,4,16,768]{3,2,1,0:T(8,128)(2,1)}), bf16[32,4,16,768]{3,2,1,0:T(8,128)(2,1)S(1)}, u32[]{:S(2)}, u32[]{:S(2)}) async-start(bf16[32,4,16,768]{3,2,1,0:T(8,128)(2,1)} %bitcast.66), calls=%async_computation.3 | async-start | bytes 6291456 | tf_op jit(solution)/shard_map/all_to_all | solution.py:516
  595.5 473.6 %reduce-scatter.8.cloned.1.call-start = ((), (), s32[]{:S(2)}) async-start(), calls=%async_computation.14 | async-start | bytes 4866048 | tf_op jit(solution)/shard_map/reduce_scatter | solution.py:553
  686.2 3.7 copy-start.8
  686.2 167.6 %all-to-all-start.2 = ((bf16[32,4,16,768]{3,2,1,0:T(8,128)(2,1)}), bf16[32,4,16,768]{3,2,1,0:T(8,128)(2,1)}, u32[]{:S(2)}, u32[]{:S(2)}) async-start(bf16[32,4,16,768]{3,2,1,0:T(8,128)(2,1)} %bitcast.65), calls=%async_computation.2 | async-start | bytes 6291456 | tf_op jit(solution)/shard_map/all_to_all | solution.py:516
  853.8 216.9 %copy-start.1 = (bf16[2048,768]{1,0:T(8,128)(2,1)S(1)}, bf16[2048,768]{1,0:T(8,128)(2,1)}, u32[]{:S(2)}) copy-start(bf16[2048,768]{1,0:T(8,128)(2,1)} %param.11) | copy-start | bytes 9437188
Sparse Core Ops, SparseCore 0:
  11.5 88.0 all-gather.7
  102.4 77.0 all-gather.9
  182.4 56.5 all-gather.11
  241.8 62.4 all-gather.13
  307.1 61.9 all-gather.15
  487.9 95.3 reduce-scatter.3
  588.9 199.3 all-reduce.3
  791.8 53.2 all-gather.17
  850.5 106.6 reduce-scatter.5
  962.6 106.4 reduce-scatter.7

commit v2 on v1

--- a/solution.py
+++ b/solution.py
@@ -17,6 +17,7 @@
 SLOTS = 2
 PAGE = 16
 LANES = 128
+GAIN_COLS = 128
 PAIRS = HEADS // 2
 ROWS = MB * BIN
 CHUNK = 768
@@ -252,9 +253,9 @@
 
 
 def rows_body(
-    spans_ref, x_ref, o_ref, dy_ref, ada_ref, wo_ref, wu_ref, wd_ref,
-    y_ref, dx1_ref, do_ref, dada_ref, go_hbm, gu_hbm, gd_hbm,
-    go_acc, gu_acc, gd_acc, hb_ref, dmlp_ref, mlp_ref, dh_ref, stage_ref, sem,
+    spans_ref, x_ref, o_ref, dy_ref, ada_ref, feat_ref, wo_ref, wu_ref, wd_ref,
+    y_ref, dx1_ref, do_ref, grads_hbm,
+    go_acc, gu_acc, gd_acc, dada_ref, hb_ref, dmlp_ref, mlp_ref, dh_ref, stage_ref, sem,
 ):
     step = pl.program_id(0)
     last = pl.num_programs(0) - 1
@@ -305,10 +306,10 @@
         t = jnp.tanh(u * (c0 + (c0 * 0.044715) * uu))
         half = 0.5 + 0.5 * t
         gb = (u * half).astype(bf16)
-        mlp_ref[...] += mm(gb, wd_ref[cols, :], NN)
-        gd_acc[cols, :] += mm(gb, dmlp_ref[...], TN)
+        mlp_ref[...] += mm(gb, wd_ref[:, cols], NN)
+        gd_acc[:, cols] += mm(gb, dmlp_ref[...], TN)
         slope = half + (u * (1.0 - t * t)) * (0.5 * c0 + (1.5 * c0 * 0.044715) * uu)
-        du = (mm(dmlp_ref[...], wd_ref[cols, :], NT) * slope).astype(bf16)
+        du = (mm(dmlp_ref[...], wd_ref[:, cols], NT) * slope).astype(bf16)
         dh_ref[...] += mm(du, wu_ref[:, cols], NT)
         gu_acc[:, cols] += mm(hb_ref[...], du, TN)
         return carry
@@ -328,25 +329,43 @@
 
     @pl.when(step == last)
     def _():
+        high = dada_ref[...].astype(bf16)
+        low = (dada_ref[...] - high.astype(f32)).astype(bf16)
+        sums = jnp.concatenate([high, low], axis=0)
+
+        def slots_grad(r, c):
+            return mm(feat_ref[:, r : r + PIECE], sums[:, c : c + D], TN)
+
+        def held(acc):
+            return lambda r, c: acc[r : r + PIECE, c : c + D]
+
         pieces = []
-        for acc, out in ((go_acc, go_hbm), (gu_acc, gu_hbm), (gd_acc, gd_hbm)):
-            for r in range(0, acc.shape[0], PIECE):
-                for c in range(0, acc.shape[1], D):
-                    at = (slice(r, r + PIECE), slice(c, c + D))
-                    pieces.append((acc.at[at], out.at[at]))
+        for piece, first, width in (
+            (held(gu_acc), 0, FF),
+            (held(gd_acc), FF, FF),
+            (held(go_acc), 2 * FF, D),
+            (slots_grad, 2 * FF + D, 3 * D),
+        ):
+            for r in range(0, D, PIECE):
+                for c in range(0, width, D):
+                    pieces.append((piece, r, c, grads_hbm.at[r : r + PIECE, first + c : first + c + D]))
         copies = [None, None]
-        for i, (acc, out) in enumerate(pieces):
+        for i, (piece, r, c, out) in enumerate(pieces):
             slot = i % 2
             if copies[slot] is not None:
                 copies[slot].wait()
-            stage_ref[slot] = acc[...].astype(bf16)
+            stage_ref[slot] = piece(r, c).astype(bf16)
             copies[slot] = pltpu.make_async_copy(stage_ref.at[slot], out, sem.at[slot])
             copies[slot].start()
         for copy in copies:
             copy.wait()
 
 
-def rows_call(spans, x, o, dy, ada, w_out, w_up, w_down):
+def columns(width, index):
+    return pl.BlockSpec((D, width), lambda *g: (0, index), pipeline_mode=pl.Buffered(1))
+
+
+def rows_call(spans, x, o, dy, ada, feat, weights):
     rows = x.shape[0]
     block = pl.BlockSpec((BLOCK, D), lambda i, s: (i, 0))
     anywhere = pl.BlockSpec(memory_space=pl.ANY)
@@ -357,15 +376,17 @@
             num_scalar_prefetch=1,
             grid=(rows // BLOCK,),
             in_specs=[
-                block, block, block, fixed((8, 3 * D)), fixed((D, D)), fixed((D, FF)), fixed((FF, D)),
+                block, block, block, fixed((8, 3 * D)), fixed((16, D)),
+                columns(D, 2 * FF // D), columns(FF, 0), columns(FF, 1),
             ],
             out_specs=[
-                block, block, block, pl.BlockSpec((8, 3 * D), lambda i, s: (0, 0)), anywhere, anywhere, anywhere,
+                block, block, block, anywhere,
             ],
             scratch_shapes=[
                 pltpu.VMEM((D, D), f32),
                 pltpu.VMEM((D, FF), f32),
-                pltpu.VMEM((FF, D), f32),
+                pltpu.VMEM((D, FF), f32),
+                pltpu.VMEM((8, 3 * D), f32),
                 pltpu.VMEM((BLOCK, D), bf16),
                 pltpu.VMEM((BLOCK, D), bf16),
                 pltpu.VMEM((BLOCK, D), f32),
@@ -378,16 +399,13 @@
             jax.ShapeDtypeStruct((rows, D), bf16),
             jax.ShapeDtypeStruct((rows, D), f32),
             jax.ShapeDtypeStruct((rows, D), bf16),
-            jax.ShapeDtypeStruct((8, 3 * D), f32),
-            jax.ShapeDtypeStruct((D, D), bf16),
-            jax.ShapeDtypeStruct((D, FF), bf16),
-            jax.ShapeDtypeStruct((FF, D), bf16),
+            jax.ShapeDtypeStruct((D, 2 * FF + 4 * D), bf16),
         ],
         compiler_params=params("arbitrary"),
         cost_estimate=pl.CostEstimate(
             flops=6 * rows * D * (D + 2 * FF), bytes_accessed=rows * D * 14, transcendentals=rows * FF
         ),
-    )(spans, x, o, dy, ada, w_out, w_up, w_down)
+    )(spans, x, o, dy, ada, feat, weights, weights, weights)
 
 
 def qkv_back_body(x_ref, dx1_ref, dq_ref, dk_ref, dv_ref, gain_ref, w_ref, dx_ref, gg_ref):
@@ -525,59 +543,62 @@
     rows_dev = x_given.shape[0]
     pages_dev = rows_dev // PAGE
     send_pos, send_order, recv_pos, recv_order = page_plan(page_deal, pages_dev, shards, device)
-    x = exchange(pages(x_given)[send_order], shards)[recv_pos].reshape(rows_dev, D)
-    dy = exchange(pages(cotangent)[send_order], shards)[recv_pos].reshape(rows_dev, D)
-
-    def gather(w):
-        return lax.all_gather(w, AXES, axis=0, tiled=True)
-
-    qkv_all = gather(w_qkv)
-    ada_ext = jnp.concatenate([w_ada, jnp.broadcast_to(norm_gain[:, None], (norm_gain.shape[0], LANES))], axis=1)
-    ada_ext = gather(ada_ext)
-    out_all, up_all, down_all = gather(w_out), gather(w_up), gather(w_down)
-    ada_all = ada_ext[:, : 3 * D]
-    gain = jnp.broadcast_to(ada_ext[:, 3 * D].astype(f32)[None, :], (8, D))
+    own = norm_gain.shape[0]
+    parts = FF // D
+    x_got = exchange(pages(x_given)[send_order], shards)
+    dy_sent, x_got = lax.optimization_barrier((pages(cotangent)[send_order], x_got))
+    dy_got = exchange(dy_sent, shards)
+    x = x_got[recv_pos].reshape(rows_dev, D)
+
+    def gather(*ws):
+        return lax.all_gather(jnp.concatenate(ws, axis=1), AXES, axis=0, tiled=True)
+
+    def reduce(g):
+        return lax.optimization_barrier(lax.psum_scatter(g, AXES, scatter_dimension=0, tiled=True))
+
+    up_own = w_up.reshape(own, shards, parts, own).transpose(0, 2, 1, 3).reshape(own, FF)
+    down_own = w_down.reshape(parts, own, D).transpose(1, 0, 2).reshape(own, FF)
+    first_all = gather(w_qkv, w_ada, jnp.broadcast_to(norm_gain[:, None], (own, LANES)))
+    second_all = gather(up_own, down_own, w_out)
+    ada_all = first_all[:, 3 * D : 6 * D]
+    gain = jnp.broadcast_to(first_all[:, 6 * D].astype(f32)[None, :], (8, D))
 
     cosine, sine, query_mask, key_mask = row_tables(seq_spans)
     time_feat = time_features(time_steps, D)
     ada_seq = jnp.dot(time_feat, ada_all, preferred_element_type=f32)
     ada_seq = jnp.concatenate([ada_seq, jnp.zeros_like(ada_seq)], axis=0)
-
-    qkv, a1 = qkv_call(x, gain, qkv_all, cosine, sine)
+    feat = jnp.concatenate([time_feat, jnp.zeros_like(time_feat)], axis=0)
+    feat = jnp.concatenate([feat, feat], axis=0)
+
+    qkv, a1 = qkv_call(x, gain, first_all, cosine, sine)
     p, o, rl = attend_call(qkv, query_mask, key_mask)
-    y, dx1, do, dada, go, gu, gd = rows_call(seq_spans, x, o, dy, ada_seq, out_all, up_all, down_all)
-
-    output = exchange(pages(y)[recv_order], shards)[send_pos].reshape(rows_dev, D)
-
-    def reduce(g):
-        return lax.psum_scatter(g, AXES, scatter_dimension=0, tiled=True)
-
-    up_grad, down_grad, out_grad = reduce(gu), reduce(gd), reduce(go)
-    slots = time_steps.shape[0]
-    steps_col = jnp.broadcast_to(time_steps.astype(f32)[:, None], (slots, LANES))
-    slot_rows = jnp.concatenate([dada[:slots], steps_col], axis=1)
-    slot_all = lax.all_gather(slot_rows, AXES, axis=0, tiled=True)
-    own = norm_gain.shape[0]
-    half = D // 2
-    feature = device * own + jnp.arange(own, dtype=jnp.int32)
-    frequency = jnp.exp((feature % half).astype(f32) * (-math.log(10000.0) / half))
-    angle = slot_all[:, 3 * D : 3 * D + 1] * frequency[None, :]
-    feat_own = jnp.where(feature[None, :] < half, jnp.cos(angle), jnp.sin(angle)).astype(bf16).astype(f32)
-    ada_grad = lax.dot_general(feat_own, slot_all[:, : 3 * D], TN, precision=lax.Precision.HIGHEST)
+    dy_got, o = lax.optimization_barrier((dy_got, o))
+    dy = dy_got[recv_pos].reshape(rows_dev, D)
+    y, dx1, do, grads = rows_call(seq_spans, x, o, dy, ada_seq, feat, second_all)
+
+    y_sent, do = lax.optimization_barrier((pages(y)[recv_order], do))
+    y_got = exchange(y_sent, shards)
+    grads = reduce(grads)
 
     dq, dk, dv = attend_back_call(qkv, do, o, rl, p, cosine, sine)
-    dx, gg = qkv_back_call(x, dx1, dq, dk, dv, gain, qkv_all)
-    input_grad = exchange(pages(dx)[recv_order], shards)[send_pos].reshape(rows_dev, D)
+    dq, y_got = lax.optimization_barrier((dq, y_got))
+    dx, gg = qkv_back_call(x, dx1, dq, dk, dv, gain, first_all)
+    dx_sent = pages(dx)[recv_order]
+    output = y_got[send_pos].reshape(rows_dev, D)
     gq = qkv_grad_call(a1, dq, dk, dv)
-    gq = jnp.concatenate([gq, jnp.broadcast_to(gg[0].astype(bf16)[:, None], (D, LANES))], axis=1)
+    gq = jnp.concatenate([gq, jnp.broadcast_to(gg[0].astype(bf16)[:, None], (D, GAIN_COLS))], axis=1)
+    gq, grads = lax.optimization_barrier((gq, grads))
     gq = reduce(gq)
+    input_grad = exchange(dx_sent, shards)[send_pos].reshape(rows_dev, D)
+    up_grad = grads[:, :FF].reshape(own, parts, shards, own).transpose(0, 2, 1, 3).reshape(own, FF)
+    down_grad = grads[:, FF : 2 * FF].reshape(own, parts, D).transpose(1, 0, 2).reshape(parts * own, D)
     return (
         output,
         input_grad,
         gq[:, 3 * D].astype(f32),
         gq[:, : 3 * D].astype(f32),
-        out_grad.astype(f32),
-        ada_grad,
+        grads[:, 2 * FF : 2 * FF + D].astype(f32),
+        grads[:, 2 * FF + D :].astype(f32),
         up_grad.astype(f32),
         down_grad.astype(f32),
     )

time: 1080 us -> 719 us (0.67)
  waiting for transfers between devices: 708 us -> 327 us
  local copies, waits for them, and re-layouts: 36 us -> 53.2 us
    all_gather x6 -> x2, waiting for transfers between devices: 156 us -> 0.01 us  [gather(): return lax.all_gather(jnp.concatenate(ws, axis=1), AXES, axis=0, tiled=True)]
    reduce_scatter x3 -> x1, waiting for transfers between devices: 209 us -> 64.4 us  [reduce(): lax.psum_scatter(g, AXES, scatter_dimension=0, tiled=True)]
    all_to_all x4, waiting for transfers between devices: 242 us -> 195 us  [exchange(): got = lax.all_to_all(sent, AXES, split_axis=0, concat_axis=0, tiled=True)]
    unnamed x11 -> x5, waiting for transfers between devices: 101 us -> 67.1 us
    convert_element_type x0 -> x5, local copies, waits for them, and re-layouts: none -> 12.9 us  [the longest x3 10.3 us: per_device(): up_grad.astype(f32)]
  transfers between devices with their start and end apart: 14 -> 8, of which waited for: 9 -> 6; matrix products, arithmetic and copies ran while one was open for 6% -> 10% of each run, Pallas kernels for 14% -> 21%
where the time goes in v2:
time: 719 us; the launch traced here: 718 us
  waiting for transfers between devices  327 us (45%)
  Pallas kernels  275 us (38%)
  local copies, waits for them, and re-layouts  53.2 us (7%)
  other arithmetic  24.6 us (3%)
  starting transfers between devices  21.1 us (3%)
  between operations  14.1 us (2%)
    all_to_all x4, waiting for transfers between devices, exchange(): got = lax.all_to_all(sent, AXES, split_axis=0, concat_axis=0, tiled=True)  195 us
    pallas_call x1, Pallas kernels, rows_call(): pl.pallas_call(rows_body, name='rows', grid_spec=pltpu.PrefetchScalarGrid...  124 us
    unnamed x5, waiting for transfers between devices  67.1 us
    pallas_call x1, Pallas kernels, attend_back_call(): pl.pallas_call(attend_back_body, name='attend_back', grid=(bins, PAIRS),...  66.1 us
    reduce_scatter x1, waiting for transfers between devices, reduce(): lax.psum_scatter(g, AXES, scatter_dimension=0, tiled=True)  64.4 us
    pallas_call x1, Pallas kernels, attend_call(): pl.pallas_call(attend_body, name='attend', grid=(bins, PAIRS), in_specs=[...  40.8 us
    all_to_all x4, starting transfers between devices, exchange(): got = lax.all_to_all(sent, AXES, split_axis=0, concat_axis=0, tiled=True)  21 us
    pallas_call x1, Pallas kernels, qkv_back_call(): pl.pallas_call(qkv_back_body, name='qkv_back', grid=(rows // blk,), in_sp...  16.6 us
  transfers between devices with their start and end apart: 8, of which 6 were waited for; matrix products, arithmetic and copies ran while one was open for 10% of the time, Pallas kernels for 21%

profile of v2, /device:TPU:0, one launch (start us, length us, event | category | flops | bytes accessed | tf_op | source)
XLA Modules:
  0.0 717.6 jit_solution(16266568687227609075)
XLA Ops:
  10.0 3.0 reshape.348
  13.0 2.2 copy.34
  19.1 2.4 gather_fusion.1
  21.5 7.3 %all-to-all-start = ((bf16[32,4,16,768]{3,2,1,0:T(8,128)(2,1)}), bf16[32,4,16,768]{3,2,1,0:T(8,128)(2,1)S(1)}, u32[]{:S(2)}, u32[]{:S(2)}) async-start(bf16[32,4,16,768]{3,2,1,0:T(8,128)(2,1)} %bitcast.72), calls=%async_computation | async-start | bytes 6291456 | tf_op jit(solution)/shard_map/all_to_all | solution.py:534
  29.6 4.4 gather_fusion
  34.3 96.4 %all-to-all-done = bf16[32,4,16,768]{3,2,1,0:T(8,128)(2,1)S(1)} async-done(((bf16[32,4,16,768]{3,2,1,0:T(8,128)(2,1)}), bf16[32,4,16,768]{3,2,1,0:T(8,128)(2,1)S(1)}, u32[]{:S(2)}, u32[]{:S(2)}) %all-to-all-start) | async-done | bytes 3145760 | tf_op jit(solution)/shard_map/all_to_all | solution.py:534
  130.7 3.9 all-to-all-start.1
  139.1 5.6 fusion.2
  144.6 2.4 gather_fusion.2
  148.7 15.2 %qkv.1 = (bf16[2048,2304]{1,0:T(8,128)(2,1)}, bf16[2048,768]{1,0:T(8,128)(2,1)}) custom-call(bf16[2048,768]{1,0:T(8,128)(2,1)} %bitcast.76, f32[8,768]{1,0:T(8,128)} %broadcast_in_dim.135.gain_ref, bf16[768,4736]{1,0:T(8,128)(2,1)} %all-gather.3.cloned.1.call-done.w_ref, f32[2048,128]{1,0:T(8,128)} %get-tuple-element.65.cos_ref, ...), custom_call_target="tpu_custom_call" | custom-call | flops 7247757312 | bytes 15728640 | tf_op jit(solution)/shard_map/qkv/pallas_call | solution.py:86
  163.9 40.8 %attend.1 = (bf16[2,12,1024,1024]{3,2,1,0:T(8,128)(2,1)}, bf16[2048,768]{1,0:T(8,128)(2,1)}, f32[2048,128]{1,0:T(8,128)}) custom-call(bf16[2048,2304]{1,0:T(8,128)(2,1)} %get-tuple-element.33.q_ref.k_ref.v_ref, bf16[2048,2304]{1,0:T(8,128)(2,1)} %get-tuple-element.33.q_ref.k_ref.v_ref, bf16[2048,2304]{1,0:T(8,128)(2,1)} %get-tuple-element.33.q_ref.k_ref.v_ref, ...), custom_call_target="tpu_custom_call" | custom-call | flops 25769803776 | bytes 50331648 | tf_op jit(solution)/shard_map/attend/pallas_call | solution.py:144
  204.7 48.8 %all-to-all-done.1 = bf16[32,4,16,768]{3,2,1,0:T(8,128)(2,1)} async-done(((bf16[32,4,16,768]{3,2,1,0:T(8,128)(2,1)}), bf16[32,4,16,768]{3,2,1,0:T(8,128)(2,1)}, u32[]{:S(2)}, u32[]{:S(2)}) %all-to-all-start.1) | async-done | bytes 3145760 | tf_op jit(solution)/shard_map/all_to_all | solution.py:534
  253.6 4.3 gather_fusion.3
  257.8 2.6 fusion
  261.1 123.6 %rows.1 = (bf16[2048,768]{1,0:T(8,128)(2,1)}, f32[2048,768]{1,0:T(8,128)}, bf16[2048,768]{1,0:T(8,128)(2,1)}, bf16[768,9216]{1,0:T(8,128)(2,1)}) custom-call(s32[4,2]{1,0:T(4,128)} %copy.36.spans_ref, bf16[2048,768]{1,0:T(8,128)(2,1)} %bitcast.77, bf16[2048,768]{1,0:T(8,128)(2,1)} %get-tuple-element.36.o_ref, bf16[2048,768]{1,0:T(8,128)(2,1)} %bitcast.82, ...), custom_call_target="tpu_custom_call" | custom-call | flops 65229815808 | bytes 22020096 | tf_op jit(solution)/shard_map/rows/pallas_call | solution.py:372
  386.6 2.4 gather_fusion.4
  389.0 3.4 all-to-all-start.2
  392.3 66.1 %attend_back.1 = (bf16[2048,768]{1,0:T(8,128)(2,1)}, bf16[2048,768]{1,0:T(8,128)(2,1)}, bf16[2048,768]{1,0:T(8,128)(2,1)}) custom-call(bf16[2048,2304]{1,0:T(8,128)(2,1)} %get-tuple-element.33.q_ref.k_ref.v_ref, bf16[2048,2304]{1,0:T(8,128)(2,1)} %get-tuple-element.33.q_ref.k_ref.v_ref, bf16[2048,2304]{1,0:T(8,128)(2,1)} %get-tuple-element.33.q_ref.k_ref.v_ref, ...), custom_call_target="tpu_custom_call" | custom-call | flops 51539607552 | bytes 50331648 | tf_op jit(solution)/shard_map/attend_back/pallas_call | solution.py:224
  458.4 40.6 %all-to-all-done.2 = bf16[32,4,16,768]{3,2,1,0:T(8,128)(2,1)S(1)} async-done(((bf16[32,4,16,768]{3,2,1,0:T(8,128)(2,1)}), bf16[32,4,16,768]{3,2,1,0:T(8,128)(2,1)S(1)}, u32[]{:S(2)}, u32[]{:S(2)}) %all-to-all-start.2) | async-done | bytes 3145760 | tf_op jit(solution)/shard_map/all_to_all | solution.py:534
  499.0 16.6 %qkv_back.1 = (bf16[2048,768]{1,0:T(8,128)(2,1)}, f32[8,768]{1,0:T(8,128)}) custom-call(bf16[2048,768]{1,0:T(8,128)(2,1)} %bitcast.78, f32[2048,768]{1,0:T(8,128)} %get-tuple-element.46.dx1_ref, bf16[2048,768]{1,0:T(8,128)(2,1)} %get-tuple-element.47.dq_ref, bf16[2048,768]{1,0:T(8,128)(2,1)} %get-tuple-element.48.dk_ref, ...), custom_call_target="tpu_custom_call" | custom-call | flops 7247757312 | bytes 22020096 | tf_op jit(solution)/shard_map/qkv_back/pallas_call | solution.py:430
  515.7 4.3 gather_fusion.6
  520.0 6.4 all-to-all-start.3
  527.2 12.7 %qkv_grad.1 = bf16[768,2304]{1,0:T(8,128)(2,1)} custom-call(bf16[2048,768]{1,0:T(8,128)(2,1)} %get-tuple-element.51.a1_ref, bf16[2048,768]{1,0:T(8,128)(2,1)} %get-tuple-element.47.dq_ref, bf16[2048,768]{1,0:T(8,128)(2,1)} %get-tuple-element.48.dk_ref, bf16[2048,768]{1,0:T(8,128)(2,1)} %get-tuple-element.49.dv_ref), custom_call_target="tpu_custom_call" | custom-call | flops 7247757312 | bytes 12582912 | tf_op jit(solution)/shard_map/qkv_grad/pallas_call | solution.py:464
  540.1 4.1 pad_maximum_fusion
  544.2 64.4 %reduce-scatter.5.cloned.1.call-done = bf16[24,9216]{1,0:T(8,128)(2,1)} async-done(((bf16[768,9216]{1,0:T(8,128)(2,1)}), bf16[24,9216]{1,0:T(8,128)(2,1)}) %reduce-scatter.5.cloned.1.call-update) | async-done | bytes 442384 | tf_op jit(solution)/shard_map/reduce_scatter | solution.py:557
  608.7 2.4 gather_fusion.5
  611.1 9.5 %all-to-all-done.3 = bf16[32,4,16,768]{3,2,1,0:T(8,128)(2,1)} async-done(((bf16[32,4,16,768]{3,2,1,0:T(8,128)(2,1)}), bf16[32,4,16,768]{3,2,1,0:T(8,128)(2,1)}, u32[]{:S(2)}, u32[]{:S(2)}) %all-to-all-start.3) | async-done | bytes 3145760 | tf_op jit(solution)/shard_map/all_to_all | solution.py:534
  620.6 4.5 gather_fusion.7
  625.1 2.3 reshape.364
  627.4 4.0 copy.37
  631.4 4.0 reshape.362
  641.1 67.1 %reduce-scatter.7.cloned.1.call-done = bf16[24,2432]{1,0:T(8,128)(2,1)} async-done(((bf16[768,2432]{1,0:T(8,128)(2,1)}), bf16[24,2432]{1,0:T(8,128)(2,1)}) %reduce-scatter.7.cloned.1.call-update) | async-done | bytes 116752
  (86 shorter events, 25.8 us)
Async XLA Ops:
  7.2 11.9 %copy-start = (bf16[2048,768]{1,0:T(8,128)(2,1)S(1)}, bf16[2048,768]{1,0:T(8,128)(2,1)}, u32[]{:S(2)}) copy-start(bf16[2048,768]{1,0:T(8,128)(2,1)} %param.11) | copy-start | bytes 9437188
  7.2 10.1 %copy-start.4 = (bf16[96,768]{1,0:T(8,128)(2,1)S(1)}, bf16[96,768]{1,0:T(8,128)(2,1)}, u32[]{:S(2)}) copy-start(bf16[96,768]{1,0:T(8,128)(2,1)} %param.18) | copy-start | bytes 442372
  7.2 10.2 %copy-start.5 = (bf16[24,768]{1,0:T(8,128)(2,1)S(1)}, bf16[24,768]{1,0:T(8,128)(2,1)}, u32[]{:S(2)}) copy-start(bf16[24,768]{1,0:T(8,128)(2,1)} %param.15) | copy-start | bytes 110596
  7.2 11.0 %copy-start.6 = (s32[4096]{0:T(1024)S(1)}, s32[4096]{0:T(1024)}, u32[]{:S(2)}) copy-start(s32[4096]{0:T(1024)} %param.21) | copy-start | bytes 49156
  7.2 139.8 %all-gather.3.cloned.1.call-start = ((), (), s32[]{:S(2)}) async-start(), calls=%async_computation.6 | async-start | bytes 7501824 | tf_op jit(solution)/shard_map/all_gather | solution.py:554
  9.9 251.2 %all-gather.5.cloned.1.call-start = ((), (), s32[]{:S(2)}) async-start(), calls=%async_computation.7 | async-start | bytes 10948608 | tf_op jit(solution)/shard_map/all_gather | solution.py:554
  21.5 7.3 %copy-start.7 = (s32[4,2]{0,1:T(2,128)S(1)}, s32[4,2]{0,1:T(2,128)}, u32[]{:S(2)}) copy-start(s32[4,2]{0,1:T(2,128)} %param.19) | copy-start | bytes 100
  21.5 109.2 %all-to-all-start = ((bf16[32,4,16,768]{3,2,1,0:T(8,128)(2,1)}), bf16[32,4,16,768]{3,2,1,0:T(8,128)(2,1)S(1)}, u32[]{:S(2)}, u32[]{:S(2)}) async-start(bf16[32,4,16,768]{3,2,1,0:T(8,128)(2,1)} %bitcast.72), calls=%async_computation | async-start | bytes 6291456 | tf_op jit(solution)/shard_map/all_to_all | solution.py:534
  29.6 4.6 copy-start.9
  130.7 122.9 %all-to-all-start.1 = ((bf16[32,4,16,768]{3,2,1,0:T(8,128)(2,1)}), bf16[32,4,16,768]{3,2,1,0:T(8,128)(2,1)}, u32[]{:S(2)}, u32[]{:S(2)}) async-start(bf16[32,4,16,768]{3,2,1,0:T(8,128)(2,1)} %bitcast.12), calls=%async_computation.1 | async-start | bytes 6291456 | tf_op jit(solution)/shard_map/all_to_all | solution.py:534
  134.6 474.1 %reduce-scatter.5.cloned.1.call-start = ((), (), s32[]{:S(2)}) async-start(), calls=%async_computation.8 | async-start | bytes 14598144 | tf_op jit(solution)/shard_map/reduce_scatter | solution.py:557
  384.7 1.9 copy-start.2
  389.0 110.1 %all-to-all-start.2 = ((bf16[32,4,16,768]{3,2,1,0:T(8,128)(2,1)}), bf16[32,4,16,768]{3,2,1,0:T(8,128)(2,1)S(1)}, u32[]{:S(2)}, u32[]{:S(2)}) async-start(bf16[32,4,16,768]{3,2,1,0:T(8,128)(2,1)} %bitcast.73), calls=%async_computation.2 | async-start | bytes 6291456 | tf_op jit(solution)/shard_map/all_to_all | solution.py:534
  520.0 100.6 %all-to-all-start.3 = ((bf16[32,4,16,768]{3,2,1,0:T(8,128)(2,1)}), bf16[32,4,16,768]{3,2,1,0:T(8,128)(2,1)}, u32[]{:S(2)}, u32[]{:S(2)}) async-start(bf16[32,4,16,768]{3,2,1,0:T(8,128)(2,1)} %bitcast.71), calls=%async_computation.3 | async-start | bytes 6291456 | tf_op jit(solution)/shard_map/all_to_all | solution.py:534
  526.4 181.7 %reduce-scatter.7.cloned.1.call-start = ((), (), s32[]{:S(2)}) async-start(), calls=%async_computation.9 | async-start | bytes 3852288
  544.2 64.5 %copy-start.8 = (s32[128]{0:T(128)S(1)}, s32[128]{0:T(128)}, u32[]{:S(2)}) copy-start(s32[128]{0:T(128)} %get-tuple-element.56) | copy-start | bytes 1540
  620.6 4.5 copy-start.3
  627.4 83.6 %copy-start.1 = (bf16[2048,768]{1,0:T(8,128)(2,1)S(1)}, bf16[2048,768]{1,0:T(8,128)(2,1)}, u32[]{:S(2)}) copy-start(bf16[2048,768]{1,0:T(8,128)(2,1)} %param.11) | copy-start | bytes 9437188
Sparse Core Ops, SparseCore 0:
  11.5 110.5 all-gather.2
  125.0 128.5 all-gather.4
  384.8 223.7 reduce-scatter.4
  614.1 93.9 reduce-scatter.6

commit v3 on v2

--- a/solution.py
+++ b/solution.py
@@ -18,6 +18,9 @@
 PAGE = 16
 LANES = 128
 GAIN_COLS = 128
+OUT_AT = 6 * D
+GAIN_AT = 7 * D
+UP_AT = 8 * D
 PAIRS = HEADS // 2
 ROWS = MB * BIN
 CHUNK = 768
@@ -377,7 +380,7 @@
             grid=(rows // BLOCK,),
             in_specs=[
                 block, block, block, fixed((8, 3 * D)), fixed((16, D)),
-                columns(D, 2 * FF // D), columns(FF, 0), columns(FF, 1),
+                columns(D, OUT_AT // D), columns(FF, UP_AT // FF), columns(FF, UP_AT // FF + 1),
             ],
             out_specs=[
                 block, block, block, anywhere,
@@ -558,10 +561,10 @@
 
     up_own = w_up.reshape(own, shards, parts, own).transpose(0, 2, 1, 3).reshape(own, FF)
     down_own = w_down.reshape(parts, own, D).transpose(1, 0, 2).reshape(own, FF)
-    first_all = gather(w_qkv, w_ada, jnp.broadcast_to(norm_gain[:, None], (own, LANES)))
-    second_all = gather(up_own, down_own, w_out)
-    ada_all = first_all[:, 3 * D : 6 * D]
-    gain = jnp.broadcast_to(first_all[:, 6 * D].astype(f32)[None, :], (8, D))
+    gain_own = jnp.broadcast_to(norm_gain[:, None], (own, UP_AT - GAIN_AT))
+    weights = gather(w_qkv, w_ada, w_out, gain_own, up_own, down_own)
+    ada_all = weights[:, 3 * D : 6 * D]
+    gain = jnp.broadcast_to(weights[:, GAIN_AT].astype(f32)[None, :], (8, D))
 
     cosine, sine, query_mask, key_mask = row_tables(seq_spans)
     time_feat = time_features(time_steps, D)
@@ -570,11 +573,11 @@
     feat = jnp.concatenate([time_feat, jnp.zeros_like(time_feat)], axis=0)
     feat = jnp.concatenate([feat, feat], axis=0)
 
-    qkv, a1 = qkv_call(x, gain, first_all, cosine, sine)
+    qkv, a1 = qkv_call(x, gain, weights, cosine, sine)
     p, o, rl = attend_call(qkv, query_mask, key_mask)
     dy_got, o = lax.optimization_barrier((dy_got, o))
     dy = dy_got[recv_pos].reshape(rows_dev, D)
-    y, dx1, do, grads = rows_call(seq_spans, x, o, dy, ada_seq, feat, second_all)
+    y, dx1, do, grads = rows_call(seq_spans, x, o, dy, ada_seq, feat, weights)
 
     y_sent, do = lax.optimization_barrier((pages(y)[recv_order], do))
     y_got = exchange(y_sent, shards)
@@ -582,12 +585,12 @@
 
     dq, dk, dv = attend_back_call(qkv, do, o, rl, p, cosine, sine)
     dq, y_got = lax.optimization_barrier((dq, y_got))
-    dx, gg = qkv_back_call(x, dx1, dq, dk, dv, gain, first_all)
+    dx, gg = qkv_back_call(x, dx1, dq, dk, dv, gain, weights)
     dx_sent = pages(dx)[recv_order]
     output = y_got[send_pos].reshape(rows_dev, D)
     gq = qkv_grad_call(a1, dq, dk, dv)
     gq = jnp.concatenate([gq, jnp.broadcast_to(gg[0].astype(bf16)[:, None], (D, GAIN_COLS))], axis=1)
-    gq, grads = lax.optimization_barrier((gq, grads))
+    gq, grads, dx_sent = lax.optimization_barrier((gq, grads, dx_sent))
     gq = reduce(gq)
     input_grad = exchange(dx_sent, shards)[send_pos].reshape(rows_dev, D)
     up_grad = grads[:, :FF].reshape(own, parts, shards, own).transpose(0, 2, 1, 3).reshape(own, FF)

time: 719 us -> 745 us (1.036)
  waiting for transfers between devices: 327 us -> 354 us
    all_gather x2 -> x1, waiting for transfers between devices: 0.01 us -> 72.4 us  [gather(): return lax.all_gather(jnp.concatenate(ws, axis=1), AXES, axis=0, tiled=True)]
    all_to_all x4, waiting for transfers between devices: 195 us -> 155 us  [exchange(): got = lax.all_to_all(sent, AXES, split_axis=0, concat_axis=0, tiled=True)]
    reduce_scatter x1, waiting for transfers between devices: 64.4 us -> 30.4 us  [reduce(): lax.psum_scatter(g, AXES, scatter_dimension=0, tiled=True)]
    unnamed x5 -> x4, waiting for transfers between devices: 67.1 us -> 96.2 us
  transfers between devices with their start and end apart: 8 -> 7, of which waited for: 6 -> 5; matrix products, arithmetic and copies ran while one was open for 10% -> 7% of each run, Pallas kernels for 21% -> 20%
where the time goes in v3:
time: 745 us; the launch traced here: 743 us
  waiting for transfers between devices  354 us (48%)
  Pallas kernels  276 us (37%)
  local copies, waits for them, and re-layouts  52.6 us (7%)
  other arithmetic  24.5 us (3%)
  starting transfers between devices  19.9 us (3%)
  between operations  14.1 us (2%)
    all_to_all x4, waiting for transfers between devices, exchange(): got = lax.all_to_all(sent, AXES, split_axis=0, concat_axis=0, tiled=True)  155 us
    pallas_call x1, Pallas kernels, rows_call(): pl.pallas_call(rows_body, name='rows', grid_spec=pltpu.PrefetchScalarGrid...  124 us
    unnamed x4, waiting for transfers between devices  96.2 us
    all_gather x1, waiting for transfers between devices, gather(): return lax.all_gather(jnp.concatenate(ws, axis=1), AXES, axis=0, tiled=True)  72.4 us
    pallas_call x1, Pallas kernels, attend_back_call(): pl.pallas_call(attend_back_body, name='attend_back', grid=(bins, PAIRS),...  66.1 us
    pallas_call x1, Pallas kernels, attend_call(): pl.pallas_call(attend_body, name='attend', grid=(bins, PAIRS), in_specs=[...  40.8 us
    reduce_scatter x1, waiting for transfers between devices, reduce(): lax.psum_scatter(g, AXES, scatter_dimension=0, tiled=True)  30.4 us
    all_to_all x4, starting transfers between devices, exchange(): got = lax.all_to_all(sent, AXES, split_axis=0, concat_axis=0, tiled=True)  19.5 us
  transfers between devices with their start and end apart: 7, of which 5 were waited for; matrix products, arithmetic and copies ran while one was open for 7% of the time, Pallas kernels for 20%

profile of v3, /device:TPU:0, one launch (start us, length us, event | category | flops | bytes accessed | tf_op | source)
XLA Modules:
  0.0 743.4 jit_solution(12314927890303127389)
XLA Ops:
  7.3 1.7 constant_dynamic-update-slice_fusion.4
  8.9 3.0 reshape.344
  11.9 2.2 copy.34
  14.1 2.1 reshape.345
  23.5 2.4 gather_fusion.1
  25.9 7.3 all-to-all-start
  33.3 4.3 gather_fusion
  37.6 114.3 %all-to-all-done = bf16[32,4,16,768]{3,2,1,0:T(8,128)(2,1)S(1)} async-done(((bf16[32,4,16,768]{3,2,1,0:T(8,128)(2,1)}), bf16[32,4,16,768]{3,2,1,0:T(8,128)(2,1)S(1)}, u32[]{:S(2)}, u32[]{:S(2)}) %all-to-all-start) | async-done | bytes 3145760 | tf_op jit(solution)/shard_map/all_to_all | solution.py:537
  153.6 5.1 all-to-all-start.1
  163.5 5.5 fusion.2
  169.1 4.3 gather_fusion.2
  173.4 72.4 %all-gather.2.cloned.1.call-done.w_ref.wo_ref.wu_ref.wd_ref = bf16[768,12288]{1,0:T(8,128)(2,1)} async-done(((bf16[24,12288]{1,0:T(8,128)(2,1)}), bf16[768,12288]{1,0:T(8,128)(2,1)}) %all-gather.2.cloned.1.call-update) | async-done | bytes 18874384 | tf_op jit(solution)/shard_map/all_gather | solution.py:557
  247.5 15.2 %qkv.1 = (bf16[2048,2304]{1,0:T(8,128)(2,1)}, bf16[2048,768]{1,0:T(8,128)(2,1)}) custom-call(bf16[2048,768]{1,0:T(8,128)(2,1)} %bitcast.69, f32[8,768]{1,0:T(8,128)} %broadcast_in_dim.135.gain_ref, bf16[768,12288]{1,0:T(8,128)(2,1)} %all-gather.2.cloned.1.call-done.w_ref.wo_ref.wu_ref.wd_ref, f32[2048,128]{1,0:T(8,128)} %get-tuple-element.67.cos_ref, ...), custom_call_target="tpu_custom_call" | custom-call | flops 7247757312 | bytes 15728640 | tf_op jit(solution)/shard_map/qkv/pallas_call | solution.py:89
  262.6 40.8 %attend.1 = (bf16[2,12,1024,1024]{3,2,1,0:T(8,128)(2,1)}, bf16[2048,768]{1,0:T(8,128)(2,1)}, f32[2048,128]{1,0:T(8,128)}) custom-call(bf16[2048,2304]{1,0:T(8,128)(2,1)} %get-tuple-element.34.q_ref.k_ref.v_ref, bf16[2048,2304]{1,0:T(8,128)(2,1)} %get-tuple-element.34.q_ref.k_ref.v_ref, bf16[2048,2304]{1,0:T(8,128)(2,1)} %get-tuple-element.34.q_ref.k_ref.v_ref, ...), custom_call_target="tpu_custom_call" | custom-call | flops 25769803776 | bytes 50331648 | tf_op jit(solution)/shard_map/attend/pallas_call | solution.py:147
  303.4 2.4 gather_fusion.3
  305.8 2.6 fusion
  309.1 123.6 %rows.1 = (bf16[2048,768]{1,0:T(8,128)(2,1)}, f32[2048,768]{1,0:T(8,128)}, bf16[2048,768]{1,0:T(8,128)(2,1)}, bf16[768,9216]{1,0:T(8,128)(2,1)}) custom-call(s32[4,2]{1,0:T(4,128)} %copy.36.spans_ref, bf16[2048,768]{1,0:T(8,128)(2,1)} %bitcast.70, bf16[2048,768]{1,0:T(8,128)(2,1)} %get-tuple-element.37.o_ref, bf16[2048,768]{1,0:T(8,128)(2,1)} %bitcast.83, ...), custom_call_target="tpu_custom_call" | custom-call | flops 65229815808 | bytes 22020096 | tf_op jit(solution)/shard_map/rows/pallas_call | solution.py:375
  432.9 1.7 copy-done.3
  434.6 2.4 gather_fusion.4
  437.0 3.2 all-to-all-start.2
  440.2 66.1 %attend_back.1 = (bf16[2048,768]{1,0:T(8,128)(2,1)}, bf16[2048,768]{1,0:T(8,128)(2,1)}, bf16[2048,768]{1,0:T(8,128)(2,1)}) custom-call(bf16[2048,2304]{1,0:T(8,128)(2,1)} %get-tuple-element.34.q_ref.k_ref.v_ref, bf16[2048,2304]{1,0:T(8,128)(2,1)} %get-tuple-element.34.q_ref.k_ref.v_ref, bf16[2048,2304]{1,0:T(8,128)(2,1)} %get-tuple-element.34.q_ref.k_ref.v_ref, ...), custom_call_target="tpu_custom_call" | custom-call | flops 51539607552 | bytes 50331648 | tf_op jit(solution)/shard_map/attend_back/pallas_call | solution.py:227
  506.4 40.6 %all-to-all-done.2 = bf16[32,4,16,768]{3,2,1,0:T(8,128)(2,1)S(1)} async-done(((bf16[32,4,16,768]{3,2,1,0:T(8,128)(2,1)}), bf16[32,4,16,768]{3,2,1,0:T(8,128)(2,1)S(1)}, u32[]{:S(2)}, u32[]{:S(2)}) %all-to-all-start.2) | async-done | bytes 3145760 | tf_op jit(solution)/shard_map/all_to_all | solution.py:537
  546.9 16.6 %qkv_back.1 = (bf16[2048,768]{1,0:T(8,128)(2,1)}, f32[8,768]{1,0:T(8,128)}) custom-call(bf16[2048,768]{1,0:T(8,128)(2,1)} %bitcast.71, f32[2048,768]{1,0:T(8,128)} %get-tuple-element.51.dx1_ref, bf16[2048,768]{1,0:T(8,128)(2,1)} %get-tuple-element.48.dq_ref, bf16[2048,768]{1,0:T(8,128)(2,1)} %get-tuple-element.49.dk_ref, ...), custom_call_target="tpu_custom_call" | custom-call | flops 7247757312 | bytes 22020096 | tf_op jit(solution)/shard_map/qkv_back/pallas_call | solution.py:433
  563.5 4.3 gather_fusion.6
  568.6 13.5 %qkv_grad.1 = bf16[768,2304]{1,0:T(8,128)(2,1)} custom-call(bf16[2048,768]{1,0:T(8,128)(2,1)} %get-tuple-element.47.a1_ref, bf16[2048,768]{1,0:T(8,128)(2,1)} %get-tuple-element.48.dq_ref, bf16[2048,768]{1,0:T(8,128)(2,1)} %get-tuple-element.49.dk_ref, bf16[2048,768]{1,0:T(8,128)(2,1)} %get-tuple-element.50.dv_ref), custom_call_target="tpu_custom_call" | custom-call | flops 7247757312 | bytes 12582912 | tf_op jit(solution)/shard_map/qkv_grad/pallas_call | solution.py:467
  582.3 4.1 pad_maximum_fusion
  586.4 30.4 %reduce-scatter.5.cloned.1.call-done = bf16[24,9216]{1,0:T(8,128)(2,1)} async-done(((bf16[768,9216]{1,0:T(8,128)(2,1)}), bf16[24,9216]{1,0:T(8,128)(2,1)}) %reduce-scatter.5.cloned.1.call-update) | async-done | bytes 442384 | tf_op jit(solution)/shard_map/reduce_scatter | solution.py:560
  616.8 3.9 all-to-all-start.3
  621.5 2.4 gather_fusion.5
  627.3 2.5 reshape.362
  633.8 95.7 %reduce-scatter.7.cloned.1.call-done = bf16[24,2432]{1,0:T(8,128)(2,1)} async-done(((bf16[768,2432]{1,0:T(8,128)(2,1)}), bf16[24,2432]{1,0:T(8,128)(2,1)}) %reduce-scatter.7.cloned.1.call-update) | async-done | bytes 116752
  732.4 4.5 gather_fusion.7
  (85 shorter events, 28.0 us)
Async XLA Ops:
  7.2 16.3 %copy-start = (bf16[2048,768]{1,0:T(8,128)(2,1)S(1)}, bf16[2048,768]{1,0:T(8,128)(2,1)}, u32[]{:S(2)}) copy-start(bf16[2048,768]{1,0:T(8,128)(2,1)} %param.11) | copy-start | bytes 9437188
  7.2 9.1 %copy-start.4 = (bf16[96,768]{1,0:T(8,128)(2,1)S(1)}, bf16[96,768]{1,0:T(8,128)(2,1)}, u32[]{:S(2)}) copy-start(bf16[96,768]{1,0:T(8,128)(2,1)} %param.18) | copy-start | bytes 442372
  7.2 9.2 %copy-start.5 = (bf16[24,2304]{1,0:T(8,128)(2,1)S(1)}, bf16[24,2304]{1,0:T(8,128)(2,1)}, u32[]{:S(2)}) copy-start(bf16[24,2304]{1,0:T(8,128)(2,1)} %param.16) | copy-start | bytes 331780
  7.2 11.2 %copy-start.8 = (bf16[24]{0:T(256)(128)(2,1)S(1)}, bf16[24]{0:T(256)(128)(2,1)}, u32[]{:S(2)}) copy-start(bf16[24]{0:T(256)(128)(2,1)} %param.13) | copy-start | bytes 148
  7.2 238.6 %all-gather.2.cloned.1.call-start = ((), (), s32[]{:S(2)}) async-start(), calls=%async_computation.6 | async-start | bytes 19464192 | tf_op jit(solution)/shard_map/all_gather | solution.py:557
  25.9 126.1 %all-to-all-start = ((bf16[32,4,16,768]{3,2,1,0:T(8,128)(2,1)}), bf16[32,4,16,768]{3,2,1,0:T(8,128)(2,1)S(1)}, u32[]{:S(2)}, u32[]{:S(2)}) async-start(bf16[32,4,16,768]{3,2,1,0:T(8,128)(2,1)} %bitcast.77), calls=%async_computation | async-start | bytes 6291456 | tf_op jit(solution)/shard_map/all_to_all | solution.py:537
  33.3 4.3 copy-start.6
  152.0 1.7 copy-start.2
  152.0 7.6 %copy-start.9 = (s32[4]{0:T(128)S(1)}, s32[4]{0:T(128)}, u32[]{:S(2)}) copy-start(s32[4]{0:T(128)} %param.20) | copy-start | bytes 52
  153.6 149.8 %all-to-all-start.1 = ((bf16[32,4,16,768]{3,2,1,0:T(8,128)(2,1)}), bf16[32,4,16,768]{3,2,1,0:T(8,128)(2,1)S(1)}, u32[]{:S(2)}, u32[]{:S(2)}) async-start(bf16[32,4,16,768]{3,2,1,0:T(8,128)(2,1)} %bitcast.15), calls=%async_computation.1 | async-start | bytes 6291456 | tf_op jit(solution)/shard_map/all_to_all | solution.py:537
  158.7 458.1 %reduce-scatter.5.cloned.1.call-start = ((), (), s32[]{:S(2)}) async-start(), calls=%async_computation.7 | async-start | bytes 14598144 | tf_op jit(solution)/shard_map/reduce_scatter | solution.py:560
  432.7 1.9 copy-start.3
  437.0 109.9 %all-to-all-start.2 = ((bf16[32,4,16,768]{3,2,1,0:T(8,128)(2,1)}), bf16[32,4,16,768]{3,2,1,0:T(8,128)(2,1)S(1)}, u32[]{:S(2)}, u32[]{:S(2)}) async-start(bf16[32,4,16,768]{3,2,1,0:T(8,128)(2,1)} %bitcast.76), calls=%async_computation.2 | async-start | bytes 6291456 | tf_op jit(solution)/shard_map/all_to_all | solution.py:537
  616.8 115.6 %all-to-all-start.3 = ((bf16[32,4,16,768]{3,2,1,0:T(8,128)(2,1)}), bf16[32,4,16,768]{3,2,1,0:T(8,128)(2,1)}, u32[]{:S(2)}, u32[]{:S(2)}) async-start(bf16[32,4,16,768]{3,2,1,0:T(8,128)(2,1)} %bitcast.75), calls=%async_computation.4 | async-start | bytes 6291456 | tf_op jit(solution)/shard_map/all_to_all | solution.py:537
  620.7 0.8 copy-start.7
  620.7 108.8 %reduce-scatter.7.cloned.1.call-start = ((), (), s32[]{:S(2)}) async-start(), calls=%async_computation.8 | async-start | bytes 3852288
  732.4 4.5 copy-start.1
Sparse Core Ops, SparseCore 0:
  20.6 225.0 all-gather.1
  432.8 183.9 reduce-scatter.4
  627.2 102.2 reduce-scatter.6

commit v4 on v2

--- a/solution.py
+++ b/solution.py
@@ -545,7 +545,8 @@
     send_pos, send_order, recv_pos, recv_order = page_plan(page_deal, pages_dev, shards, device)
     own = norm_gain.shape[0]
     parts = FF // D
-    x_got = exchange(pages(x_given)[send_order], shards)
+    x_sent, w_up, w_down = lax.optimization_barrier((pages(x_given)[send_order], w_up, w_down))
+    x_got = exchange(x_sent, shards)
     dy_sent, x_got = lax.optimization_barrier((pages(cotangent)[send_order], x_got))
     dy_got = exchange(dy_sent, shards)
     x = x_got[recv_pos].reshape(rows_dev, D)
@@ -572,7 +573,7 @@
 
     qkv, a1 = qkv_call(x, gain, first_all, cosine, sine)
     p, o, rl = attend_call(qkv, query_mask, key_mask)
-    dy_got, o = lax.optimization_barrier((dy_got, o))
+    dy_got, o, ada_seq = lax.optimization_barrier((dy_got, o, ada_seq))
     dy = dy_got[recv_pos].reshape(rows_dev, D)
     y, dx1, do, grads = rows_call(seq_spans, x, o, dy, ada_seq, feat, second_all)
 
@@ -587,7 +588,7 @@
     output = y_got[send_pos].reshape(rows_dev, D)
     gq = qkv_grad_call(a1, dq, dk, dv)
     gq = jnp.concatenate([gq, jnp.broadcast_to(gg[0].astype(bf16)[:, None], (D, GAIN_COLS))], axis=1)
-    gq, grads = lax.optimization_barrier((gq, grads))
+    gq, grads, dx_sent = lax.optimization_barrier((gq, grads, dx_sent))
     gq = reduce(gq)
     input_grad = exchange(dx_sent, shards)[send_pos].reshape(rows_dev, D)
     up_grad = grads[:, :FF].reshape(own, parts, shards, own).transpose(0, 2, 1, 3).reshape(own, FF)

time: 719 us -> 694 us (0.965)
  waiting for transfers between devices: 327 us -> 313 us
  local copies, waits for them, and re-layouts: 53.2 us -> 41.5 us
    reduce_scatter x1, waiting for transfers between devices: 64.4 us -> 30.4 us  [reduce(): lax.psum_scatter(g, AXES, scatter_dimension=0, tiled=True)]
    unnamed x5, waiting for transfers between devices: 67.1 us -> 96.1 us
    all_to_all x4, waiting for transfers between devices: 195 us -> 186 us  [exchange(): got = lax.all_to_all(sent, AXES, split_axis=0, concat_axis=0, tiled=True)]
  transfers between devices with their start and end apart: 8 -> 8, of which waited for: 6 -> 5; matrix products, arithmetic and copies ran while one was open for 10% -> 9% of each run, Pallas kernels for 21% -> 22%
where the time goes in v4:
time: 694 us; the launch traced here: 692 us
  waiting for transfers between devices  313 us (45%)
  Pallas kernels  276 us (40%)
  local copies, waits for them, and re-layouts  41.5 us (6%)
  other arithmetic  26.2 us (4%)
  starting transfers between devices  19.3 us (3%)
  between operations  14.1 us (2%)
    all_to_all x4, waiting for transfers between devices, exchange(): got = lax.all_to_all(sent, AXES, split_axis=0, concat_axis=0, tiled=True)  186 us
    pallas_call x1, Pallas kernels, rows_call(): pl.pallas_call(rows_body, name='rows', grid_spec=pltpu.PrefetchScalarGrid...  124 us
    unnamed x5, waiting for transfers between devices  96.1 us
    pallas_call x1, Pallas kernels, attend_back_call(): pl.pallas_call(attend_back_body, name='attend_back', grid=(bins, PAIRS),...  66.1 us
    pallas_call x1, Pallas kernels, attend_call(): pl.pallas_call(attend_body, name='attend', grid=(bins, PAIRS), in_specs=[...  40.9 us
    reduce_scatter x1, waiting for transfers between devices, reduce(): lax.psum_scatter(g, AXES, scatter_dimension=0, tiled=True)  30.4 us
    all_to_all x4, starting transfers between devices, exchange(): got = lax.all_to_all(sent, AXES, split_axis=0, concat_axis=0, tiled=True)  18.9 us
    pallas_call x1, Pallas kernels, qkv_back_call(): pl.pallas_call(qkv_back_body, name='qkv_back', grid=(rows // blk,), in_sp...  16.6 us
  transfers between devices with their start and end apart: 8, of which 5 were waited for; matrix products, arithmetic and copies ran while one was open for 9% of the time, Pallas kernels for 22%

profile of v4, /device:TPU:0, one launch (start us, length us, event | category | flops | bytes accessed | tf_op | source)
XLA Modules:
  0.0 692.4 jit_solution(3349532715960361479)
XLA Ops:
  8.1 1.7 pad_maximum_fusion.2
  11.5 2.4 gather_fusion.1
  17.4 7.3 %all-to-all-start = ((bf16[32,4,16,768]{3,2,1,0:T(8,128)(2,1)}), bf16[32,4,16,768]{3,2,1,0:T(8,128)(2,1)S(1)}, u32[]{:S(2)}, u32[]{:S(2)}) async-start(bf16[32,4,16,768]{3,2,1,0:T(8,128)(2,1)} %bitcast.72), calls=%async_computation | async-start | bytes 6291456 | tf_op jit(solution)/shard_map/all_to_all | solution.py:534
  24.8 4.4 gather_fusion
  29.9 98.9 %all-to-all-done = bf16[32,4,16,768]{3,2,1,0:T(8,128)(2,1)S(1)} async-done(((bf16[32,4,16,768]{3,2,1,0:T(8,128)(2,1)}), bf16[32,4,16,768]{3,2,1,0:T(8,128)(2,1)S(1)}, u32[]{:S(2)}, u32[]{:S(2)}) %all-to-all-start) | async-done | bytes 3145760 | tf_op jit(solution)/shard_map/all_to_all | solution.py:534
  128.9 3.7 all-to-all-start.1
  134.5 1.5 convert_reduce_fusion
  137.3 5.6 fusion.2
  142.9 2.4 gather_fusion.2
  145.3 2.6 fusion
  150.2 15.2 %qkv.1 = (bf16[2048,2304]{1,0:T(8,128)(2,1)}, bf16[2048,768]{1,0:T(8,128)(2,1)}) custom-call(bf16[2048,768]{1,0:T(8,128)(2,1)} %bitcast.76, f32[8,768]{1,0:T(8,128)} %broadcast_in_dim.135.gain_ref, bf16[768,4736]{1,0:T(8,128)(2,1)} %all-gather.3.cloned.1.call-done.w_ref, f32[2048,128]{1,0:T(8,128)} %get-tuple-element.75.cos_ref, ...), custom_call_target="tpu_custom_call" | custom-call | flops 7247757312 | bytes 15728640 | tf_op jit(solution)/shard_map/qkv/pallas_call | solution.py:86
  165.4 40.9 %attend.1 = (bf16[2,12,1024,1024]{3,2,1,0:T(8,128)(2,1)}, bf16[2048,768]{1,0:T(8,128)(2,1)}, f32[2048,128]{1,0:T(8,128)}) custom-call(bf16[2048,2304]{1,0:T(8,128)(2,1)} %get-tuple-element.39.q_ref.k_ref.v_ref, bf16[2048,2304]{1,0:T(8,128)(2,1)} %get-tuple-element.39.q_ref.k_ref.v_ref, bf16[2048,2304]{1,0:T(8,128)(2,1)} %get-tuple-element.39.q_ref.k_ref.v_ref, ...), custom_call_target="tpu_custom_call" | custom-call | flops 25769803776 | bytes 50331648 | tf_op jit(solution)/shard_map/attend/pallas_call | solution.py:144
  206.3 46.8 %all-to-all-done.1 = bf16[32,4,16,768]{3,2,1,0:T(8,128)(2,1)} async-done(((bf16[32,4,16,768]{3,2,1,0:T(8,128)(2,1)}), bf16[32,4,16,768]{3,2,1,0:T(8,128)(2,1)}, u32[]{:S(2)}, u32[]{:S(2)}) %all-to-all-start.1) | async-done | bytes 3145760 | tf_op jit(solution)/shard_map/all_to_all | solution.py:534
  253.1 4.3 gather_fusion.3
  257.4 123.6 %rows.1 = (bf16[2048,768]{1,0:T(8,128)(2,1)}, f32[2048,768]{1,0:T(8,128)}, bf16[2048,768]{1,0:T(8,128)(2,1)}, bf16[768,9216]{1,0:T(8,128)(2,1)}) custom-call(s32[4,2]{1,0:T(4,128)} %copy.36.spans_ref, bf16[2048,768]{1,0:T(8,128)(2,1)} %bitcast.77, bf16[2048,768]{1,0:T(8,128)(2,1)} %get-tuple-element.42.o_ref, bf16[2048,768]{1,0:T(8,128)(2,1)} %bitcast.82, ...), custom_call_target="tpu_custom_call" | custom-call | flops 65229815808 | bytes 22020096 | tf_op jit(solution)/shard_map/rows/pallas_call | solution.py:372
  381.2 1.7 copy-done.2
  382.9 2.4 gather_fusion.4
  385.3 3.7 all-to-all-start.2
  389.0 66.1 %attend_back.1 = (bf16[2048,768]{1,0:T(8,128)(2,1)}, bf16[2048,768]{1,0:T(8,128)(2,1)}, bf16[2048,768]{1,0:T(8,128)(2,1)}) custom-call(bf16[2048,2304]{1,0:T(8,128)(2,1)} %get-tuple-element.39.q_ref.k_ref.v_ref, bf16[2048,2304]{1,0:T(8,128)(2,1)} %get-tuple-element.39.q_ref.k_ref.v_ref, bf16[2048,2304]{1,0:T(8,128)(2,1)} %get-tuple-element.39.q_ref.k_ref.v_ref, ...), custom_call_target="tpu_custom_call" | custom-call | flops 51539607552 | bytes 50331648 | tf_op jit(solution)/shard_map/attend_back/pallas_call | solution.py:224
  455.1 40.6 %all-to-all-done.2 = bf16[32,4,16,768]{3,2,1,0:T(8,128)(2,1)S(1)} async-done(((bf16[32,4,16,768]{3,2,1,0:T(8,128)(2,1)}), bf16[32,4,16,768]{3,2,1,0:T(8,128)(2,1)S(1)}, u32[]{:S(2)}, u32[]{:S(2)}) %all-to-all-start.2) | async-done | bytes 3145760 | tf_op jit(solution)/shard_map/all_to_all | solution.py:534
  495.7 16.6 %qkv_back.1 = (bf16[2048,768]{1,0:T(8,128)(2,1)}, f32[8,768]{1,0:T(8,128)}) custom-call(bf16[2048,768]{1,0:T(8,128)(2,1)} %bitcast.78, f32[2048,768]{1,0:T(8,128)} %get-tuple-element.59.dx1_ref, bf16[2048,768]{1,0:T(8,128)(2,1)} %get-tuple-element.56.dq_ref, bf16[2048,768]{1,0:T(8,128)(2,1)} %get-tuple-element.57.dk_ref, ...), custom_call_target="tpu_custom_call" | custom-call | flops 7247757312 | bytes 22020096 | tf_op jit(solution)/shard_map/qkv_back/pallas_call | solution.py:430
  512.3 4.3 gather_fusion.6
  517.4 13.5 %qkv_grad.1 = bf16[768,2304]{1,0:T(8,128)(2,1)} custom-call(bf16[2048,768]{1,0:T(8,128)(2,1)} %get-tuple-element.55.a1_ref, bf16[2048,768]{1,0:T(8,128)(2,1)} %get-tuple-element.56.dq_ref, bf16[2048,768]{1,0:T(8,128)(2,1)} %get-tuple-element.57.dk_ref, bf16[2048,768]{1,0:T(8,128)(2,1)} %get-tuple-element.58.dv_ref), custom_call_target="tpu_custom_call" | custom-call | flops 7247757312 | bytes 12582912 | tf_op jit(solution)/shard_map/qkv_grad/pallas_call | solution.py:464
  531.1 4.1 pad_maximum_fusion
  535.2 30.4 %reduce-scatter.5.cloned.1.call-done = bf16[24,9216]{1,0:T(8,128)(2,1)} async-done(((bf16[768,9216]{1,0:T(8,128)(2,1)}), bf16[24,9216]{1,0:T(8,128)(2,1)}) %reduce-scatter.5.cloned.1.call-update) | async-done | bytes 442384 | tf_op jit(solution)/shard_map/reduce_scatter | solution.py:558
  565.5 4.2 all-to-all-start.3
  570.4 2.4 gather_fusion.5
  576.2 2.5 reshape.362
  581.1 1.6 slice_convert_fusion.3
  582.7 95.8 %reduce-scatter.7.cloned.1.call-done = bf16[24,2432]{1,0:T(8,128)(2,1)} async-done(((bf16[768,2432]{1,0:T(8,128)(2,1)}), bf16[24,2432]{1,0:T(8,128)(2,1)}) %reduce-scatter.7.cloned.1.call-update) | async-done | bytes 116752
  679.8 1.6 slice_convert_fusion.2
  681.4 4.5 gather_fusion.7
  (86 shorter events, 20.9 us)
Async XLA Ops:
  7.2 4.3 copy-start
  7.2 138.1 %all-gather.3.cloned.1.call-start = ((), (), s32[]{:S(2)}) async-start(), calls=%async_computation.6 | async-start | bytes 7501824 | tf_op jit(solution)/shard_map/all_gather | solution.py:555
  9.8 247.6 %all-gather.5.cloned.1.call-start = ((), (), s32[]{:S(2)}) async-start(), calls=%async_computation.7 | async-start | bytes 10948608 | tf_op jit(solution)/shard_map/all_gather | solution.py:555
  11.5 2.4 copy-start.3
  13.9 2.7 copy-start.4
  13.9 2.8 copy-start.5
  17.4 111.4 %all-to-all-start = ((bf16[32,4,16,768]{3,2,1,0:T(8,128)(2,1)}), bf16[32,4,16,768]{3,2,1,0:T(8,128)(2,1)S(1)}, u32[]{:S(2)}, u32[]{:S(2)}) async-start(bf16[32,4,16,768]{3,2,1,0:T(8,128)(2,1)} %bitcast.72), calls=%async_computation | async-start | bytes 6291456 | tf_op jit(solution)/shard_map/all_to_all | solution.py:534
  24.8 4.5 copy-start.7
  24.8 4.7 copy-start.6
  128.9 4.4 copy-start.9
  128.9 124.2 %all-to-all-start.1 = ((bf16[32,4,16,768]{3,2,1,0:T(8,128)(2,1)}), bf16[32,4,16,768]{3,2,1,0:T(8,128)(2,1)}, u32[]{:S(2)}, u32[]{:S(2)}) async-start(bf16[32,4,16,768]{3,2,1,0:T(8,128)(2,1)} %bitcast.12), calls=%async_computation.1 | async-start | bytes 6291456 | tf_op jit(solution)/shard_map/all_to_all | solution.py:534
  132.6 433.0 %reduce-scatter.5.cloned.1.call-start = ((), (), s32[]{:S(2)}) async-start(), calls=%async_computation.8 | async-start | bytes 14598144 | tf_op jit(solution)/shard_map/reduce_scatter | solution.py:558
  381.0 1.9 copy-start.2
  385.3 110.5 %all-to-all-start.2 = ((bf16[32,4,16,768]{3,2,1,0:T(8,128)(2,1)}), bf16[32,4,16,768]{3,2,1,0:T(8,128)(2,1)S(1)}, u32[]{:S(2)}, u32[]{:S(2)}) async-start(bf16[32,4,16,768]{3,2,1,0:T(8,128)(2,1)} %bitcast.73), calls=%async_computation.2 | async-start | bytes 6291456 | tf_op jit(solution)/shard_map/all_to_all | solution.py:534
  565.5 115.8 %all-to-all-start.3 = ((bf16[32,4,16,768]{3,2,1,0:T(8,128)(2,1)}), bf16[32,4,16,768]{3,2,1,0:T(8,128)(2,1)}, u32[]{:S(2)}, u32[]{:S(2)}) async-start(bf16[32,4,16,768]{3,2,1,0:T(8,128)(2,1)} %bitcast.71), calls=%async_computation.4 | async-start | bytes 6291456 | tf_op jit(solution)/shard_map/all_to_all | solution.py:534
  569.7 0.7 copy-start.8
  569.7 108.7 %reduce-scatter.7.cloned.1.call-start = ((), (), s32[]{:S(2)}) async-start(), calls=%async_computation.9 | async-start | bytes 3852288
  681.4 4.5 copy-start.1
Sparse Core Ops, SparseCore 0:
  11.5 110.7 all-gather.2
  125.2 128.4 all-gather.4
  381.1 184.3 reduce-scatter.4
  575.9 102.5 reduce-scatter.6
